TPU v7x, 512 devices: a whole 4x4x16 slice. The times are simulated.
512 devices in a mesh: gx: 8 (over z_hi, x), gy: 8 (over y, core), ta: 8 (over z_lo).
Axes of the slice: x: 4, y: 4, z: 16 (z_hi: 2, z_lo: 8; z = z_hi * 8 + z_lo), core: 2. Of those that a mesh axis runs over, the one named last changes fastest.
Arguments:
- frames: bfloat16 [64, 64, 512, 128], P('ta', 'gx', 'gy'), may hold values from -6 to 6
- in_weight: bfloat16 [3, 3, 128, 128], replicated, may hold values from -0.1875 to 0.1875
- out_weight: bfloat16 [3, 3, 128, 128], replicated, may hold values from -0.1875 to 0.1875
- decays: float32 [64, 128], P('ta'), may hold values from 0.05 to 0.999, as said below
Outputs:
- mixed_frames: bfloat16 [64, 64, 512, 128], P('ta', 'gx', 'gy')
Inputs may be any that keep to these rules, and one draw needn't show every extreme that they name: `decays`: every factor lies strictly between 0 and 1.
All inputs are finite; a program needn't handle non-finite values.
Results may differ from a plain program's by a relative error of at most 0.0031.
Values may be sent and summed in bfloat16 or wider, within the bound.
A program may use at most 64 MiB of HBM per device.

v0:
```python
import jax
import jax.numpy as jnp
from jax import lax
from jax.sharding import PartitionSpec as P


def padded_2(cells, sides, width):
    for axis, dim in sides:
        count = lax.axis_size(axis)
        ends = count - 1
        head = lax.slice_in_dim(cells, 0, width, axis=dim)
        tail = lax.slice_in_dim(cells, cells.shape[dim] - width, cells.shape[dim], axis=dim)
        cells = jnp.concatenate(
            [
                lax.ppermute(tail, axis, [(i, (i + 1) % count) for i in range(ends)]),
                cells,
                lax.ppermute(head, axis, [((i + 1) % count, i) for i in range(ends)]),
            ],
            axis=dim,
        )
    return cells


def entering(value, axis, join, neutral):
    count, mine = (lax.axis_size(axis), lax.axis_index(axis))
    pieces = jax.tree.map(lambda part: lax.all_gather(part, axis), value)
    so_far = jax.tree.map(
        lambda part, zero: jnp.full_like(part, 0) + jnp.asarray(zero, part.dtype), value, neutral
    )

    def step(position, so_far):
        longer = join(so_far, jax.tree.map(lambda part: part[position], pieces))
        return jax.tree.map(lambda new, old: jnp.where(position < mine, new, old), longer, so_far)

    return lax.fori_loop(0, count - 1, step, so_far)


def convolve(padded, weight, height, across):
    summed = None
    for row_off in range(3):
        for col_off in range(3):
            partial_term = jnp.einsum(
                "fhwc,cp->fhwp",
                padded[:, row_off : row_off + height, col_off : col_off + across, :],
                weight[row_off, col_off],
                preferred_element_type=jnp.float32,
            )
            summed = partial_term if summed is None else summed + partial_term
    return summed


def chain_step(earlier, latter):
    return (earlier[0] * latter[0], latter[0] * earlier[1] + latter[1])


def advance(carry, inputs):
    running, current = carry
    factors, drive = inputs
    running = running * factors
    current = factors * current + drive
    return ((running, current), (running, current))


def on_device(frames, in_weight, out_weight, decays):
    height = frames.shape[1]
    across = frames.shape[2]
    padded = padded_2(frames, (("gx", 1), ("gy", 2)), 1)
    driven = convolve(padded, in_weight, height, across)
    scaled = jnp.sqrt(1.0 - decays * decays)[:, None, None, :] * driven
    start_carry = (
        jnp.ones((decays.shape[1],), jnp.float32),
        jnp.zeros(scaled.shape[1:], jnp.float32),
    )
    running, partial_states = lax.scan(advance, start_carry, (decays, scaled))[1]
    incoming = entering((running[-1], partial_states[-1]), "ta", chain_step, start_carry)
    states = partial_states + running[:, None, None, :] * incoming[1][None]
    rounded = states.astype(jnp.bfloat16)
    state_pad = padded_2(rounded, (("gx", 1), ("gy", 2)), 1)
    mixed = convolve(state_pad, out_weight, height, across)
    return (frames.astype(jnp.float32) + jax.nn.gelu(mixed)).astype(jnp.bfloat16)


def solution(mesh):
    placed = (P("ta", "gx", "gy", None), P(), P(), P("ta", None))
    return jax.shard_map(
        on_device, mesh=mesh, in_specs=placed, out_specs=P("ta", "gx", "gy", None), check_vma=False
    )
```

profile of v0, /device:TPU:7, one launch (start us, length us, event | category | flops | bytes accessed | tf_op | source)
XLA Modules:
  0.0 200.3 jit_solution(5003152059966657380)
XLA Ops:
  6.5 1.8 fusion.109
  8.3 15.3 %collective-permute-start = (bf16[8,1,64,128]{3,2,1,0:T(8,128)(2,1)}, bf16[8,1,64,128]{3,2,1,0:T(8,128)(2,1)S(1)}, u32[]{:S(2)}, u32[]{:S(2)}) collective-permute-start(bf16[8,1,64,128]{3,2,1,0:T(8,128)(2,1)} %get-tuple-element.218), channel_id=1, source_target_pairs={{0,64},{64,128},{128,192},{192,256},{256,320},{320,384},{384,448},... | collective-permute-start | bytes 393224 | tf_op jit(solution)/shard_map/ppermute | solution.py:15
  23.7 1.9 collective-permute-start.1
  25.6 1.6 fusion.72
  27.3 0.0 copy-start.1
  27.3 0.0 collective-permute-done
  27.4 0.1 constant_dynamic-update-slice_fusion.1
  27.5 13.3 %collective-permute-done.1 = bf16[8,1,64,128]{3,2,1,0:T(8,128)(2,1)} collective-permute-done((bf16[8,1,64,128]{3,2,1,0:T(8,128)(2,1)}, bf16[8,1,64,128]{3,2,1,0:T(8,128)(2,1)}, u32[]{:S(2)}, u32[]{:S(2)}) %collective-permute-start.1) | collective-permute-done | bytes 131104 | tf_op jit(solution)/shard_map/ppermute | solution.py:17
  40.8 0.9 constant_dynamic-update-slice_fusion
  41.7 0.1 fusion.107
  41.8 4.0 %collective-permute-start.3 = (bf16[8,10,1,128]{3,2,1,0:T(2,128)(2,1)S(1)}, bf16[8,10,1,128]{3,2,1,0:T(2,128)(2,1)S(1)}, u32[]{:S(2)}, u32[]{:S(2)}) collective-permute-start(bf16[8,10,1,128]{3,2,1,0:T(2,128)(2,1)S(1)} %get-tuple-element.214), channel_id=1, source_target_pairs={{8,0},{16,8},{24,16},{32,24},{40,32},{48,40},{56,48},{9,1},{17,9},... | collective-permute-start | bytes 61448 | tf_op jit(solution)/shard_map/ppermute | solution.py:17
  45.8 3.1 %collective-permute-start.2 = (bf16[8,10,1,128]{3,2,1,0:T(2,128)(2,1)S(1)}, bf16[8,10,1,128]{3,2,1,0:T(2,128)(2,1)S(1)}, u32[]{:S(2)}, u32[]{:S(2)}) collective-permute-start(bf16[8,10,1,128]{3,2,1,0:T(2,128)(2,1)S(1)} %get-tuple-element.215), channel_id=1, source_target_pairs={{0,8},{8,16},{16,24},{24,32},{32,40},{40,48},{48,56},{1,9},{9,17},... | collective-permute-start | bytes 61448 | tf_op jit(solution)/shard_map/ppermute | solution.py:15
  48.9 0.4 fusion.12
  49.4 1.3 fusion.16
  50.7 0.0 collective-permute-done.3
  50.7 0.4 fusion.29
  51.1 0.4 fusion.32
  51.6 0.0 collective-permute-done.2
  51.6 0.4 fusion.35
  52.0 0.4 fusion.38
  52.5 0.4 fusion.56
  52.9 2.6 %add_multiply_fusion = f32[8,8,64,128]{3,2,1,0:T(8,128)} fusion(f32[8,8,64,128]{3,2,1,0:T(8,128)S(1)} %fusion.16, f32[8,8,64,128]{3,2,1,0:T(8,128)S(1)} %fusion.56, f32[8,8,64,128]{3,2,1,0:T(8,128)S(1)} %fusion.29, f32[8,8,64,128]{3,2,1,0:T(8,128)S(1)} %fusion.72, f32[8,8,64,128]{3,2,1,0:T(8,128)S(1)} %fusion.35, f32[8,8,64,128]{3,2,1,0:T(8,128)S(1)} %fusion.32, ...), kind=kOutput, calls=%fused_computation.21 | convolution fusion | flops 141033472 | bytes 20262912 | tf_op jit(solution)/shard_map/fhwc,cp->fhwp/dot_general | solution.py:42
  55.5 14.5 %while.31 = (s32[]{:T(128)}, f32[128]{0:T(128)S(1)}, f32[8,64,128]{2,1,0:T(8,128)S(1)}, f32[8,128]{1,0:T(8,128)S(1)}, f32[8,8,64,128]{3,2,1,0:T(8,128)}, /*index...) while((s32[]{:T(128)}, f32[128]{0:T(128)S(1)}, ...), condition=%wide.region_1.2_spmd.clone, body=%wide.region_0.1_spmd.clone.sunk | while | flops 196867 | bytes 1052784 | solution.py:74
  55.5 1.8 bitcast_dynamic-update-slice_fusion.2
  57.3 1.8 bitcast_dynamic-update-slice_fusion.2
  59.2 1.8 bitcast_dynamic-update-slice_fusion.2
  61.0 1.8 bitcast_dynamic-update-slice_fusion.2
  62.8 1.8 bitcast_dynamic-update-slice_fusion.2
  64.6 1.8 bitcast_dynamic-update-slice_fusion.2
  66.4 1.8 bitcast_dynamic-update-slice_fusion.2
  68.2 1.8 bitcast_dynamic-update-slice_fusion.2
  70.0 1.7 slice.170
  71.7 0.0 all-gather.3.cloned.1.call-update
  71.7 30.6 %all-gather = f32[8,1,128]{2,1,0:T(1,128)S(1)} all-gather(f32[1,1,128]{2,1,0:T(1,128)S(1)} %slice_bitcast_fusion), channel_id=1, replica_groups=mesh['gx'=8,'gy'=8,'ta'=8] {'ta'}, dimensions={0}, use_global_device_ids=true | all-gather | bytes 4608 | tf_op jit(solution)/shard_map/all_gather | solution.py:26
  102.3 35.6 %all-gather.3.cloned.1.call-done = f32[8,8,64,128]{3,2,1,0:T(8,128)} async-done(((f32[1,8,64,128]{3,2,1,0:T(8,128)}), f32[8,8,64,128]{3,2,1,0:T(8,128)}) %all-gather.3.cloned.1.call-update) | async-done | bytes 2097168 | tf_op jit(solution)/shard_map/all_gather | solution.py:26
  137.9 8.3 %while.32 = (s32[]{:T(128)}, f32[8,64,128]{2,1,0:T(8,128)S(1)}, s32[]{:T(128)}, f32[8,128]{1,0:T(8,128)S(1)}, f32[8,8,64,128]{3,2,1,0:T(8,128)}, /*index=5*/s32[]{:T(128)}, s32[]{:T(128)}) while((s32[]{:T(128)}, f32[8,64,128]{2,1,0:T(8,128)S(1)}, s32[]{:T(128)}, f32[8,128]{1,0:T(8,128)S(1)}, f32[8,8,64,128]{3,2,1,0:T(8,128)}, ...), condition=%wide.region_3.4_spmd.clone, body=%wide.region_2.3_spmd.clone.sunk | while | flops 262148 | bytes 788073 | solution.py:35
  137.9 1.1 fusion.115
  139.1 1.2 fusion.115
  140.3 1.2 fusion.115
  141.5 1.2 fusion.115
  142.6 1.2 fusion.115
  143.8 1.2 fusion.115
  145.0 1.2 fusion.115
  146.2 0.0 copy-start.2
  146.2 1.9 add_convert_fusion
  148.2 8.9 %collective-permute-start.4 = (bf16[8,1,64,128]{3,2,1,0:T(8,128)(2,1)S(1)}, bf16[8,1,64,128]{3,2,1,0:T(8,128)(2,1)S(1)}, u32[]{:S(2)}, u32[]{:S(2)}) collective-permute-start(bf16[8,1,64,128]{3,2,1,0:T(8,128)(2,1)S(1)} %get-tuple-element.216), channel_id=1, source_target_pairs={{0,64},{64,128},{128,192},{192,256},{256,320},{320,384},{384,448},... | collective-permute-start | bytes 393224 | tf_op jit(solution)/shard_map/ppermute | solution.py:15
  157.0 1.9 collective-permute-start.5
  159.0 0.4 fusion.62
  159.4 0.0 collective-permute-done.4
  159.4 14.3 %collective-permute-done.5 = bf16[8,1,64,128]{3,2,1,0:T(8,128)(2,1)S(1)} collective-permute-done((bf16[8,1,64,128]{3,2,1,0:T(8,128)(2,1)S(1)}, bf16[8,1,64,128]{3,2,1,0:T(8,128)(2,1)S(1)}, u32[]{:S(2)}, u32[]{:S(2)}) %collective-permute-start.5) | collective-permute-done | bytes 131104 | tf_op jit(solution)/shard_map/ppermute | solution.py:17
  173.7 0.1 pad_maximum_fusion.7
  173.8 8.7 %collective-permute-start.6 = (bf16[8,10,1,128]{3,2,1,0:T(2,128)(2,1)S(1)}, bf16[8,10,1,128]{3,2,1,0:T(2,128)(2,1)S(1)}, u32[]{:S(2)}, u32[]{:S(2)}) collective-permute-start(bf16[8,10,1,128]{3,2,1,0:T(2,128)(2,1)S(1)} %get-tuple-element.213), channel_id=1, source_target_pairs={{0,8},{8,16},{16,24},{24,32},{32,40},{40,48},{48,56},{1,9},{9,17},... | collective-permute-start | bytes 61448 | tf_op jit(solution)/shard_map/ppermute | solution.py:15
  182.5 1.9 collective-permute-start.7
  184.4 0.4 fusion.20
  184.8 0.4 fusion.24
  185.3 0.0 collective-permute-done.6
  185.3 2.5 %collective-permute-done.7 = bf16[8,10,1,128]{3,2,1,0:T(2,128)(2,1)S(1)} collective-permute-done((bf16[8,10,1,128]{3,2,1,0:T(2,128)(2,1)S(1)}, bf16[8,10,1,128]{3,2,1,0:T(2,128)(2,1)S(1)}, u32[]{:S(2)}, u32[]{:S(2)}) %collective-permute-start.7) | collective-permute-done | bytes 20512 | tf_op jit(solution)/shard_map/ppermute | solution.py:17
  187.8 0.8 pad_maximum_fusion
  188.7 0.4 fusion.44
  189.1 0.4 fusion.48
  189.5 0.4 fusion.46
  189.9 0.4 fusion.50
  190.4 0.4 fusion.52
  190.8 2.7 %fusion.11 = bf16[8,8,64,128]{3,2,1,0:T(8,128)(2,1)} fusion(f32[8,8,64,128]{3,2,1,0:T(8,128)S(1)} %fusion.24, f32[8,8,64,128]{3,2,1,0:T(8,128)S(1)} %fusion.44, f32[8,8,64,128]{3,2,1,0:T(8,128)S(1)} %fusion.46, f32[8,8,64,128]{3,2,1,0:T(8,128)S(1)} %fusion.62, f32[8,8,64,128]{3,2,1,0:T(8,128)S(1)} %fusion.48, f32[8,8,64,128]{3,2,1,0:T(8,128)S(1)} %fusion.50, ...), kind=kOutput, calls=%fused_computation.19 | convolution fusion | flops 144179200 | bytes 19955712 | tf_op jit(solution)/shard_map/fhwc,cp->fhwp/dot_general | solution.py:42
  (39 shorter events, 0.4 us)
Async XLA Ops:
  6.5 20.8 %copy-start = (bf16[8,8,64,128]{3,2,1,0:T(8,128)(2,1)S(1)}, bf16[8,8,64,128]{3,2,1,0:T(8,128)(2,1)}, u32[]{:S(2)}) copy-start(bf16[8,8,64,128]{3,2,1,0:T(8,128)(2,1)} %param.8) | copy-start | bytes 3145732
  6.5 20.7 %copy-start.3 = (f32[8,128]{1,0:T(8,128)S(1)}, f32[8,128]{1,0:T(8,128)}, u32[]{:S(2)}) copy-start(f32[8,128]{1,0:T(8,128)} %param.11) | copy-start | bytes 12292
  6.5 131.4 %all-gather.3.cloned.1.call-start = ((), (), s32[]{:S(2)}) async-start(), calls=%async_computation | async-start | bytes 2359296 | tf_op jit(solution)/shard_map/all_gather | solution.py:26
  8.3 19.0 %collective-permute-start = (bf16[8,1,64,128]{3,2,1,0:T(8,128)(2,1)}, bf16[8,1,64,128]{3,2,1,0:T(8,128)(2,1)S(1)}, u32[]{:S(2)}, u32[]{:S(2)}) collective-permute-start(bf16[8,1,64,128]{3,2,1,0:T(8,128)(2,1)} %get-tuple-element.218), channel_id=1, source_target_pairs={{0,64},{64,128},{128,192},{192,256},{256,320},{320,384},{384,448},... | collective-permute-start | bytes 393224 | tf_op jit(solution)/shard_map/ppermute | solution.py:15
  23.7 17.1 %collective-permute-start.1 = (bf16[8,1,64,128]{3,2,1,0:T(8,128)(2,1)}, bf16[8,1,64,128]{3,2,1,0:T(8,128)(2,1)}, u32[]{:S(2)}, u32[]{:S(2)}) collective-permute-start(bf16[8,1,64,128]{3,2,1,0:T(8,128)(2,1)} %get-tuple-element.219), channel_id=1, source_target_pairs={{64,0},{128,64},{192,128},{256,192},{320,256},{384,320},{448,384},... | collective-permute-start | bytes 393224 | tf_op jit(solution)/shard_map/ppermute | solution.py:17
  27.3 21.6 %copy-start.1 = (bf16[3,3,128,128]{3,2,1,0:T(8,128)(2,1)S(1)}, bf16[3,3,128,128]{3,2,1,0:T(8,128)(2,1)}, u32[]{:S(2)}) copy-start(bf16[3,3,128,128]{3,2,1,0:T(8,128)(2,1)} %param.9) | copy-start | bytes 884740
  41.8 8.9 %collective-permute-start.3 = (bf16[8,10,1,128]{3,2,1,0:T(2,128)(2,1)S(1)}, bf16[8,10,1,128]{3,2,1,0:T(2,128)(2,1)S(1)}, u32[]{:S(2)}, u32[]{:S(2)}) collective-permute-start(bf16[8,10,1,128]{3,2,1,0:T(2,128)(2,1)S(1)} %get-tuple-element.214), channel_id=1, source_target_pairs={{8,0},{16,8},{24,16},{32,24},{40,32},{48,40},{56,48},{9,1},{17,9},... | collective-permute-start | bytes 61448 | tf_op jit(solution)/shard_map/ppermute | solution.py:17
  45.8 5.8 %collective-permute-start.2 = (bf16[8,10,1,128]{3,2,1,0:T(2,128)(2,1)S(1)}, bf16[8,10,1,128]{3,2,1,0:T(2,128)(2,1)S(1)}, u32[]{:S(2)}, u32[]{:S(2)}) collective-permute-start(bf16[8,10,1,128]{3,2,1,0:T(2,128)(2,1)S(1)} %get-tuple-element.215), channel_id=1, source_target_pairs={{0,8},{8,16},{16,24},{24,32},{32,40},{40,48},{48,56},{1,9},{9,17},... | collective-permute-start | bytes 61448 | tf_op jit(solution)/shard_map/ppermute | solution.py:15
  146.2 12.8 %copy-start.2 = (bf16[3,3,128,128]{3,2,1,0:T(8,128)(2,1)S(1)}, bf16[3,3,128,128]{3,2,1,0:T(8,128)(2,1)}, u32[]{:S(2)}) copy-start(bf16[3,3,128,128]{3,2,1,0:T(8,128)(2,1)} %param.10) | copy-start | bytes 884740
  148.2 11.2 %collective-permute-start.4 = (bf16[8,1,64,128]{3,2,1,0:T(8,128)(2,1)S(1)}, bf16[8,1,64,128]{3,2,1,0:T(8,128)(2,1)S(1)}, u32[]{:S(2)}, u32[]{:S(2)}) collective-permute-start(bf16[8,1,64,128]{3,2,1,0:T(8,128)(2,1)S(1)} %get-tuple-element.216), channel_id=1, source_target_pairs={{0,64},{64,128},{128,192},{192,256},{256,320},{320,384},{384,448},... | collective-permute-start | bytes 393224 | tf_op jit(solution)/shard_map/ppermute | solution.py:15
  157.0 16.6 %collective-permute-start.5 = (bf16[8,1,64,128]{3,2,1,0:T(8,128)(2,1)S(1)}, bf16[8,1,64,128]{3,2,1,0:T(8,128)(2,1)S(1)}, u32[]{:S(2)}, u32[]{:S(2)}) collective-permute-start(bf16[8,1,64,128]{3,2,1,0:T(8,128)(2,1)S(1)} %get-tuple-element.217), channel_id=1, source_target_pairs={{64,0},{128,64},{192,128},{256,192},{320,256},{384,320},{448,384},... | collective-permute-start | bytes 393224 | tf_op jit(solution)/shard_map/ppermute | solution.py:17
  173.8 11.5 %collective-permute-start.6 = (bf16[8,10,1,128]{3,2,1,0:T(2,128)(2,1)S(1)}, bf16[8,10,1,128]{3,2,1,0:T(2,128)(2,1)S(1)}, u32[]{:S(2)}, u32[]{:S(2)}) collective-permute-start(bf16[8,10,1,128]{3,2,1,0:T(2,128)(2,1)S(1)} %get-tuple-element.213), channel_id=1, source_target_pairs={{0,8},{8,16},{16,24},{24,32},{32,40},{40,48},{48,56},{1,9},{9,17},... | collective-permute-start | bytes 61448 | tf_op jit(solution)/shard_map/ppermute | solution.py:15
  182.5 5.3 %collective-permute-start.7 = (bf16[8,10,1,128]{3,2,1,0:T(2,128)(2,1)S(1)}, bf16[8,10,1,128]{3,2,1,0:T(2,128)(2,1)S(1)}, u32[]{:S(2)}, u32[]{:S(2)}) collective-permute-start(bf16[8,10,1,128]{3,2,1,0:T(2,128)(2,1)S(1)} %get-tuple-element.212), channel_id=1, source_target_pairs={{8,0},{16,8},{24,16},{32,24},{40,32},{48,40},{56,48},{9,1},{17,9},... | collective-permute-start | bytes 61448 | tf_op jit(solution)/shard_map/ppermute | solution.py:17
Sparse Core Ops, SparseCore 0:
  71.8 66.0 all-gather.2
where the time goes:
time: 201 us; the launch traced here: 200 us
  waiting for transfers between devices  65.7 us (33%)
  starting transfers between devices  45.8 us (23%)
  blocking collectives  30.6 us (15%)
  other arithmetic  25.2 us (13%)
  matrix products  14.2 us (7%)
  between operations  13.7 us (7%)
  local copies, waits for them, and re-layouts  4.88 us (2%)
    ppermute x4, starting transfers between devices, padded_2(): lax.ppermute(tail, axis, [(i, (i + 1) % count) for i in range(ends)])  36 us
    all_gather x1, waiting for transfers between devices, entering(): pieces = jax.tree.map(lambda part: lax.all_gather(part, axis), value)  35.6 us
    all_gather x1, blocking collectives, entering(): pieces = jax.tree.map(lambda part: lax.all_gather(part, axis), value)  30.6 us
    ppermute x4, waiting for transfers between devices, padded_2(): lax.ppermute(head, axis, [((i + 1) % count, i) for i in range(ends)])  30.1 us
    dot_general x18, matrix products, convolve(): jnp.einsum('fhwc,cp->fhwp', padded[:, row_off:row_off + height, col_off:c...  14.2 us
    dynamic_update_slice x8, other arithmetic, on_device(): lax.scan(advance, start_carry, (decays, scaled))[1]  14.2 us
    ppermute x4, starting transfers between devices, padded_2(): lax.ppermute(head, axis, [((i + 1) % count, i) for i in range(ends)])  9.77 us
    select_n x7, other arithmetic, step(): jnp.where(position < mine, new, old)  8.06 us
  transfers between devices with their start and end apart: 9, of which 4 were waited for; matrix products, arithmetic and copies ran while one was open for 3% of the time, Pallas kernels for 0%

commit v1 on v0

v1 whole, which is shorter than its diff:
```python
import functools

import jax
import jax.numpy as jnp
from jax import lax
from jax.experimental import pallas as pl
from jax.experimental.pallas import tpu as pltpu
from jax.sharding import PartitionSpec as P

MESH = pl.DeviceIdType.MESH
PAD = 8
F32 = jnp.float32
BF16 = jnp.bfloat16


def both(a, b):
    return jnp.logical_and(a, b)


def banded(dst, src):
    chans = src.shape[2]
    wide = src.shape[3]
    for i in range(4):
        for b in range(3):
            for o in range(2):
                at = (pl.ds(i * chans, chans), pl.ds((2 * b + o) * wide, wide))
                tap = i - o
                dst[at] = src[tap, b] if 0 <= tap <= 2 else jnp.zeros((chans, wide), BF16)


def conv_pair(rows, w, first):
    steps, cols, chans = rows[0].shape
    flat = jnp.concatenate([row.reshape(steps * cols, chans) for row in rows], axis=1)
    depth = flat.shape[1]
    wide = w.shape[1] // 3

    def part(b):
        block = w[pl.ds(first * chans, depth), pl.ds(b * wide, wide)]
        return jnp.dot(flat, block, preferred_element_type=F32).reshape(steps, cols, wide)

    total = part(1)
    total = total + pltpu.roll(part(0), 1, 1)
    return total + pltpu.roll(part(2), cols - 1, 1)


def kernel(
    x_hbm, wi_ref, wo_ref, dec, out, xp, wi, wo, u, st, prod, cin, cout, cup, cdn,
    loc, col_s, col_r, row_s, row_r, ch_s, ch_r, up_s, up_r, dn_s, dn_r,
):
    steps, height, width, chans = x_hbm.shape
    cols = width + 2 * PAD
    ext = height + 2
    g, h, k = lax.axis_index("gx"), lax.axis_index("gy"), lax.axis_index("ta")
    up, dn = g > 0, g < lax.axis_size("gx") - 1
    lf, rt = h > 0, h < lax.axis_size("gy") - 1
    pv, nx = k > 0, k < lax.axis_size("ta") - 1

    bar = pltpu.get_barrier_semaphore()
    partners = [
        (lf, (g, h - 1, k)), (rt, (g, h + 1, k)), (up, (g - 1, h, k)), (dn, (g + 1, h, k)),
        (pv, (g, h, k - 1)), (nx, (g, h, k + 1)),
        (both(up, pv), (g - 1, h, k - 1)), (both(up, nx), (g - 1, h, k + 1)),
        (both(dn, pv), (g + 1, h, k - 1)), (both(dn, nx), (g + 1, h, k + 1)),
    ]
    for there, device in partners:

        @pl.when(there)
        def _(device=device):
            pl.semaphore_signal(bar, inc=1, device_id=device, device_id_type=MESH)

    own = pltpu.make_async_copy(
        x_hbm, xp.at[:, pl.ds(2, height), pl.ds(PAD, width), :], loc.at[0]
    )
    own.start()

    @pl.when(jnp.logical_not(up))
    def _():
        xp[:, 0:2] = jnp.zeros((steps, 2, cols, chans), BF16)

    @pl.when(jnp.logical_not(dn))
    def _():
        xp[:, height + 2 : height + 4] = jnp.zeros((steps, 2, cols, chans), BF16)

    @pl.when(jnp.logical_not(lf))
    def _():
        xp[:, 2 : height + 2, 0:PAD] = jnp.zeros((steps, height, PAD, chans), BF16)

    @pl.when(jnp.logical_not(rt))
    def _():
        xp[:, 2 : height + 2, cols - PAD : cols] = jnp.zeros((steps, height, PAD, chans), BF16)

    @pl.when(jnp.logical_not(pv))
    def _():
        cin[...] = jnp.zeros(cin.shape, BF16)

    @pl.when(jnp.logical_not(both(pv, up)))
    def _():
        cup[...] = jnp.zeros(cup.shape, BF16)

    @pl.when(jnp.logical_not(both(pv, dn)))
    def _():
        cdn[...] = jnp.zeros(cdn.shape, BF16)

    banded(wi, wi_ref)
    banded(wo, wo_ref)
    running = dec[0:1, :]
    prod[0:1, :] = running
    for t in range(1, steps):
        running = running * dec[t : t + 1, :]
        prod[t : t + 1, :] = running

    count = sum(there.astype(jnp.int32) for there, _ in partners)
    pl.semaphore_wait(bar, count)

    def remote(src, dst, ss, rs, device):
        return pltpu.make_async_remote_copy(
            src_ref=src, dst_ref=dst, send_sem=ss, recv_sem=rs, device_id=device, device_id_type=MESH
        )

    mid = pl.ds(2, height)
    to_lf = remote(
        x_hbm.at[:, :, pl.ds(0, PAD), :], xp.at[:, mid, pl.ds(cols - PAD, PAD), :],
        col_s.at[0], col_r.at[1], (g, h - 1, k),
    )
    to_rt = remote(
        x_hbm.at[:, :, pl.ds(width - PAD, PAD), :], xp.at[:, mid, pl.ds(0, PAD), :],
        col_s.at[1], col_r.at[0], (g, h + 1, k),
    )
    to_up = remote(
        xp.at[:, pl.ds(2, 2)], xp.at[:, pl.ds(height + 2, 2)], row_s.at[0], row_r.at[1], (g - 1, h, k)
    )
    to_dn = remote(
        xp.at[:, pl.ds(height, 2)], xp.at[:, pl.ds(0, 2)], row_s.at[1], row_r.at[0], (g + 1, h, k)
    )
    pl.when(lf)(to_lf.start)
    pl.when(rt)(to_rt.start)
    own.wait()
    pl.when(lf)(to_rt.wait_recv)
    pl.when(rt)(to_lf.wait_recv)
    pl.when(up)(to_up.start)
    pl.when(dn)(to_dn.start)

    def local_states(e, rows, first, add):
        y = conv_pair(rows, wi, first)
        for o in range(2):
            state = None
            for t in range(steps):
                decay = dec[t : t + 1, :]
                drive = jnp.sqrt(1.0 - decay * decay) * y[t, :, o * chans : (o + 1) * chans]
                state = drive if state is None else decay * state + drive
                u[e + o, t] = u[e + o, t] + state if add else state

    def chain_copy(e):
        return remote(cout.at[e], cin.at[e], ch_s.at[e], ch_r.at[e], (g, h, k + 1))

    def down_copy(e):
        i = e - height
        return remote(cout.at[e], cup.at[i], up_s.at[i], up_r.at[i], (g + 1, h, k + 1))

    def up_copy(e):
        return remote(cout.at[e], cdn.at[e], dn_s.at[e], dn_r.at[e], (g - 1, h, k + 1))

    def pass_on(e, extra):
        pl.when(pv)(chain_copy(e).wait_recv)

        @pl.when(nx)
        def _():
            carried = prod[steps - 1 : steps, :] * cin[e].astype(F32) + u[e, steps - 1]
            cout[e] = carried.astype(BF16)
            chain_copy(e).start()
            if extra is not None:
                pl.when(extra[0])(extra[1](e).start)

    def finish(e, carried):
        for t in range(steps):
            st[e, t] = (u[e, t] + prod[t : t + 1, :] * carried).astype(BF16)

    local_states(height, [xp[:, height], xp[:, height + 1]], 0, False)
    local_states(0, [xp[:, 2], xp[:, 3]], 2, False)

    def inner(i, _):
        e = 2 * i
        local_states(e, [xp[:, e + j] for j in range(4)], 0, False)
        return 0

    lax.fori_loop(1, height // 2, inner, 0)
    for e in (height, height + 1):
        pass_on(e, (dn, down_copy))
    for e in (0, 1):
        pass_on(e, (up, up_copy))

    def link(e, _):
        pass_on(e, None)
        finish(e, cin[e].astype(F32))
        return 0

    lax.fori_loop(2, height, link, 0)

    def trim(first, rows):
        @pl.when(jnp.logical_not(lf))
        def _():
            st[first : first + rows, :, 0:PAD] = jnp.zeros((rows, steps, PAD, chans), BF16)

        @pl.when(jnp.logical_not(rt))
        def _():
            st[first : first + rows, :, cols - PAD : cols] = jnp.zeros((rows, steps, PAD, chans), BF16)

    def mix(r):
        y = conv_pair([st[r + j] for j in range(4)], wo, 0)
        for o in range(2):
            mixed = y[:, PAD : PAD + width, o * chans : (o + 1) * chans]
            held = xp[:, r + o + 2].astype(F32)[:, PAD : PAD + width]
            out[:, r + o] = (held + jax.nn.gelu(mixed)).astype(BF16)

    trim(2, height - 2)

    def inner_out(i, _):
        mix(2 * i)
        return 0

    lax.fori_loop(1, height // 2 - 1, inner_out, 0)

    pl.when(up)(to_dn.wait_recv)
    local_states(0, [xp[:, 0], xp[:, 1]], 0, True)
    pl.when(dn)(to_up.wait_recv)
    local_states(height, [xp[:, height + 2], xp[:, height + 3]], 2, True)
    for e in (0, 1):
        pl.when(both(pv, up))(down_copy(height + e).wait_recv)
        finish(e, cin[e].astype(F32) + cup[e].astype(F32))
    for e in (0, 1):
        pl.when(both(pv, dn))(up_copy(e).wait_recv)
        finish(height + e, cin[height + e].astype(F32) + cdn[e].astype(F32))
    trim(0, 2)
    trim(height, 2)

    @pl.when(jnp.logical_not(up))
    def _():
        st[0] = jnp.zeros((steps, cols, chans), BF16)

    @pl.when(jnp.logical_not(dn))
    def _():
        st[ext - 1] = jnp.zeros((steps, cols, chans), BF16)

    mix(0)
    mix(height - 2)

    pl.when(lf)(to_lf.wait_send)
    pl.when(rt)(to_rt.wait_send)
    pl.when(up)(to_up.wait_send)
    pl.when(dn)(to_dn.wait_send)
    for e in (height, height + 1):
        pl.when(both(nx, dn))(down_copy(e).wait_send)
    for e in (0, 1):
        pl.when(both(nx, up))(up_copy(e).wait_send)

    @pl.when(nx)
    def _():
        def sent(e, _):
            chain_copy(e).wait_send()
            return 0

        lax.fori_loop(0, ext, sent, 0)


def on_device(frames, in_weight, out_weight, decays):
    steps, height, width, chans = frames.shape
    cols, ext = width + 2 * PAD, height + 2
    dma = pltpu.SemaphoreType.DMA
    vmem = pl.BlockSpec(memory_space=pltpu.VMEM)
    return pl.pallas_call(
        kernel,
        out_shape=jax.ShapeDtypeStruct(frames.shape, BF16),
        in_specs=[pl.BlockSpec(memory_space=pl.ANY), vmem, vmem, vmem],
        out_specs=vmem,
        scratch_shapes=[
            pltpu.VMEM((steps, height + 4, cols, chans), BF16),
            pltpu.VMEM((4 * chans, 6 * chans), BF16),
            pltpu.VMEM((4 * chans, 6 * chans), BF16),
            pltpu.VMEM((ext, steps, cols, chans), F32),
            pltpu.VMEM((ext, steps, cols, chans), BF16),
            pltpu.VMEM((steps, chans), F32),
            pltpu.VMEM((ext, cols, chans), BF16),
            pltpu.VMEM((ext, cols, chans), BF16),
            pltpu.VMEM((2, cols, chans), BF16),
            pltpu.VMEM((2, cols, chans), BF16),
            dma((1,)), dma((2,)), dma((2,)), dma((2,)), dma((2,)),
            dma((ext,)), dma((ext,)), dma((2,)), dma((2,)), dma((2,)), dma((2,)),
        ],
        compiler_params=pltpu.CompilerParams(
            collective_id=0, has_side_effects=True, vmem_limit_bytes=60 << 20
        ),
        name="layer",
    )(frames, in_weight, out_weight, decays)


def solution(mesh):
    placed = (P("ta", "gx", "gy", None), P(), P(), P("ta", None))
    return jax.shard_map(
        on_device, mesh=mesh, in_specs=placed, out_specs=P("ta", "gx", "gy", None), check_vma=False
    )
```

time: 201 us -> 60.4 us (0.30)
  the two profiles are of different devices: /device:TPU:7 before, /device:TPU:55 now
where the time goes in v1:
time: 60.4 us; the launch traced here: 60.2 us
  Pallas kernels  57.9 us (96%)
  local copies, waits for them, and re-layouts  2.26 us (4%)
    pallas_call x1, Pallas kernels, on_device(): pl.pallas_call(kernel, out_shape=jax.ShapeDtypeStruct(frames.shape, BF16)...  57.9 us
    unnamed x1, local copies, waits for them, and re-layouts  2.26 us

profile of v1, /device:TPU:55, one launch (start us, length us, event | category | flops | bytes accessed | tf_op | source)
XLA Modules:
  0.0 60.2 jit_solution(8285057299106041312)
XLA Ops:
  0.0 57.9 %layer.1 = bf16[8,8,64,128]{3,2,1,0:T(8,128)(2,1)} custom-call(bf16[8,8,64,128]{3,2,1,0:T(8,128)(2,1)} %x_hbm.1, bf16[3,3,128,128]{3,2,1,0:T(8,128)(2,1)} %wi_ref.1, bf16[3,3,128,128]{3,2,1,0:T(8,128)(2,1)} %wo_ref.1, f32[8,128]{1,0:T(8,128)} %dec.1), custom_call_target="tpu_custom_call" | custom-call | tf_op jit(solution)/shard_map/layer/pallas_call | solution.py:270
  57.9 2.3 %copy.6 = bf16[8,8,64,128]{3,2,1,0:T(8,128)(2,1)} copy(bf16[8,8,64,128]{3,2,1,0:T(8,128)(2,1)} %layer.1) | data formatting | bytes 2097152

commit v2 on v1

v2 whole, which is shorter than its diff:
```python
import functools

import jax
import jax.numpy as jnp
from jax import lax
from jax.experimental import pallas as pl
from jax.experimental.pallas import tpu as pltpu
from jax.sharding import PartitionSpec as P

MESH = pl.DeviceIdType.MESH
PAD = 8
F32 = jnp.float32
BF16 = jnp.bfloat16


def both(a, b):
    return jnp.logical_and(a, b)


def banded(dst, src):
    chans = src.shape[2]
    wide = src.shape[3]
    for i in range(4):
        for b in range(3):
            for o in range(2):
                at = (pl.ds(i * chans, chans), pl.ds((2 * b + o) * wide, wide))
                tap = i - o
                dst[at] = src[tap, b] if 0 <= tap <= 2 else jnp.zeros((chans, wide), BF16)


def conv_pair(rows, w, first):
    steps, cols, chans = rows[0].shape
    flat = jnp.concatenate([row.reshape(steps * cols, chans) for row in rows], axis=1)
    depth = flat.shape[1]
    wide = w.shape[1] // 3

    def part(b):
        block = w[pl.ds(pl.multiple_of(first * chans, chans), depth), pl.ds(b * wide, wide)]
        return jnp.dot(flat, block, preferred_element_type=F32).reshape(steps, cols, wide)

    total = part(1)
    total = total + pltpu.roll(part(0), 1, 1)
    return total + pltpu.roll(part(2), cols - 1, 1)


def kernel(
    x_hbm, wi_hbm, wo_hbm, dec_hbm, out, xp, wi_ref, wo_ref, dec, wi, wo, u, st, prod, cin, cout, cx, rb, last,
    far_ok, far_sem, loc, col_s, col_r, row_s, row_r, ch_s, ch_r, bd_s, bd_r, pc_s, pc_r, rl_s, rl_r,
):
    steps, height, width, chans = x_hbm.shape
    cols = width + 2 * PAD
    ext = height + 2
    half = lax.axis_size("gx") // 2
    span = steps // half
    g, h, k = lax.axis_index("gx"), lax.axis_index("gy"), lax.axis_index("ta")
    up, dn = g > 0, g < 2 * half - 1
    lf, rt = h > 0, h < lax.axis_size("gy") - 1
    pv, nx = k > 0, k < lax.axis_size("ta") - 1
    low = g < half
    m = jnp.where(low, g, 2 * half - 1 - g)
    cross = m == half - 1
    inner, outer = jnp.where(low, g + 1, g - 1), jnp.where(low, g - 1, g + 1)
    has_outer = m > 0
    far = 2 * half - 1 - g
    up_near, dn_near = both(up, g != half), both(dn, g != half - 1)

    q = lax.axis_size("ta") // 2
    early = k < q

    def collector(at):
        return jnp.where(at < q, at + q, at)

    bar = pltpu.get_barrier_semaphore()
    signals = [
        (cross, (far, h, collector(k))), (both(cross, pv), (far, h, collector(k - 1))),
        (both(cross, early), (g, h, k + q)),
        (lf, (g, h - 1, k)), (rt, (g, h + 1, k)), (pv, (g, h, k - 1)),
        (has_outer, (outer, h, k)), (jnp.logical_not(cross), (inner, h, k)),
        (both(has_outer, pv), (outer, h, k - 1)), (both(pv, jnp.logical_not(cross)), (inner, h, k - 1)),
        (m < half - 2, (jnp.where(low, half - 1, half), h, k)),
    ]
    for there, device in signals:

        @pl.when(there)
        def _(device=device):
            pl.semaphore_signal(bar, inc=1, device_id=device, device_id_type=MESH)

    own = pltpu.make_async_copy(
        x_hbm, xp.at[:, pl.ds(2, height), pl.ds(PAD, width), :], loc.at[0]
    )
    own.start()
    loads = [
        pltpu.make_async_copy(src, dst, loc.at[i + 1])
        for i, (src, dst) in enumerate(((wi_hbm, wi_ref), (dec_hbm, dec), (wo_hbm, wo_ref)))
    ]
    for load in loads:
        load.start()

    @pl.when(jnp.logical_not(up))
    def _():
        xp[:, 0:2] = jnp.zeros((steps, 2, cols, chans), BF16)

    @pl.when(jnp.logical_not(dn))
    def _():
        xp[:, height + 2 : height + 4] = jnp.zeros((steps, 2, cols, chans), BF16)

    @pl.when(jnp.logical_not(lf))
    def _():
        xp[:, 2 : height + 2, 0:PAD] = jnp.zeros((steps, height, PAD, chans), BF16)

    @pl.when(jnp.logical_not(rt))
    def _():
        xp[:, 2 : height + 2, cols - PAD : cols] = jnp.zeros((steps, height, PAD, chans), BF16)

    @pl.when(jnp.logical_not(pv))
    def _():
        cin[...] = jnp.zeros(cin.shape, BF16)

    @pl.when(jnp.logical_not(both(pv, up)))
    def _():
        cx[0:2] = jnp.zeros((2, cols, chans), BF16)

    @pl.when(jnp.logical_not(both(pv, dn)))
    def _():
        cx[2:4] = jnp.zeros((2, cols, chans), BF16)

    def num(flag):
        return flag.astype(jnp.int32)

    count = num(lf) + num(rt) + (1 + num(nx)) * (num(has_outer) + num(jnp.logical_not(cross))) + num(nx)
    count = count + num(cross) * (half - 2) + num(both(cross, jnp.logical_not(early))) * (4 + num(nx))
    pl.semaphore_wait(bar, count)

    def tell_relays():
        for i in range(half - 1):
            pl.semaphore_signal(
                far_sem, inc=1, device_id=(jnp.where(low, i, 2 * half - 1 - i), h, k), device_id_type=MESH
            )

    @pl.when(both(cross, jnp.logical_not(early)))
    def _():
        pl.semaphore_signal(far_ok, inc=1, device_id=(g, h, k - q), device_id_type=MESH)
        tell_relays()

    def remote(src, dst, ss, rs, device):
        return pltpu.make_async_remote_copy(
            src_ref=src, dst_ref=dst, send_sem=ss, recv_sem=rs, device_id=device, device_id_type=MESH
        )

    mid = pl.ds(2, height)
    to_lf = remote(
        x_hbm.at[:, :, pl.ds(0, PAD), :], xp.at[:, mid, pl.ds(cols - PAD, PAD), :],
        col_s.at[0], col_r.at[1], (g, h - 1, k),
    )
    to_rt = remote(
        x_hbm.at[:, :, pl.ds(width - PAD, PAD), :], xp.at[:, mid, pl.ds(0, PAD), :],
        col_s.at[1], col_r.at[0], (g, h + 1, k),
    )
    to_up = remote(
        xp.at[:, pl.ds(2, 2)], xp.at[:, pl.ds(height + 2, 2)], row_s.at[0], row_r.at[1], (g - 1, h, k)
    )
    to_dn = remote(
        xp.at[:, pl.ds(height, 2)], xp.at[:, pl.ds(0, 2)], row_s.at[1], row_r.at[0], (g + 1, h, k)
    )
    leave, land = jnp.where(low, height, 2), jnp.where(low, 0, height + 2)

    def piece(i):
        return remote(
            xp.at[pl.ds(span * i, span), pl.ds(leave, 2)], rb, pc_s.at[i], rl_r.at[0],
            (jnp.where(low, i, 2 * half - 1 - i), h, k),
        )

    def landing(i, src, ss):
        return remote(
            src, xp.at[pl.ds(span * i, span), pl.ds(land, 2)], ss, pc_r.at[i],
            (jnp.where(low, half, half - 1), h, k),
        )

    direct = landing(half - 1, xp.at[pl.ds(span * (half - 1), span), pl.ds(leave, 2)], pc_s.at[half - 1])
    forward = landing(m, rb, rl_s.at[0])

    pl.when(lf)(to_lf.start)
    pl.when(rt)(to_rt.start)
    for load in loads:
        load.wait()
    banded(wi, wi_ref)
    banded(wo, wo_ref)
    running = dec[0:1, :]
    prod[0:1, :] = running
    for t in range(1, steps):
        running = running * dec[t : t + 1, :]
        prod[t : t + 1, :] = running
    own.wait()
    pl.when(lf)(to_rt.wait_recv)
    pl.when(rt)(to_lf.wait_recv)

    @pl.when(cross)
    def _():
        for i in range(half - 1):
            piece(i).start()

    @pl.when(both(cross, jnp.logical_not(early)))
    def _():
        direct.start()

    pl.when(up_near)(to_up.start)
    pl.when(dn_near)(to_dn.start)

    def local_states(e, rows, first, add):
        y = conv_pair(rows, wi, first)
        for o in range(2):
            state = None
            for t in range(steps):
                decay = dec[t : t + 1, :]
                drive = jnp.sqrt(1.0 - decay * decay) * y[t, :, o * chans : (o + 1) * chans]
                state = drive if state is None else decay * state + drive
                u[e + o, t] = u[e + o, t] + state if add else state
            if not add:
                last[e + o] = state

    def chain_copy(e):
        return remote(cout.at[e], cin.at[e], ch_s.at[e], ch_r.at[e], (g, h, k + 1))

    def down_copy(o):
        return remote(cout.at[height + o], cx.at[o], bd_s.at[o], bd_r.at[o], (g + 1, h, k + 1))

    def up_copy(o):
        return remote(cout.at[o], cx.at[2 + o], bd_s.at[2 + o], bd_r.at[2 + o], (g - 1, h, k + 1))

    def send_row(e, value):
        cout[e] = value.astype(BF16)
        chain_copy(e).start()

    def send_edge(e, o):
        pl.when(both(e == 0, up))(up_copy(o).start)
        pl.when(both(e > 0, dn))(down_copy(o).start)

    def finish(e, carried):
        for t in range(steps):
            st[e, t] = (u[e, t] + prod[t : t + 1, :] * carried).astype(BF16)

    def edge(i):
        return jnp.where((i == 0) == low, height, 0)

    def held_back(i):
        return both(both(cross, early), i == 0)

    head = jnp.logical_not(pv)

    def own_edge(i, _):
        e = edge(i)
        r = jnp.where(e == 0, 2, height)
        local_states(e, [xp[:, r], xp[:, r + 1]], jnp.where(e == 0, 2, 0), False)

        @pl.when(both(head, nx))
        def _():
            for o in range(2):
                send_row(e + o, last[e + o])
                pl.when(jnp.logical_not(held_back(i)))(lambda o=o: send_edge(e, o))

        return 0

    lax.fori_loop(0, 2, own_edge, 0)

    def own_inner(i, _):
        e = 2 * i
        local_states(e, [xp[:, e + j] for j in range(4)], 0, False)

        @pl.when(both(head, nx))
        def _():
            for o in range(2):
                send_row(e + o, last[e + o])

        return 0

    lax.fori_loop(1, height // 2, own_inner, 0)

    def add_halo(e):
        r = jnp.where(e == 0, 0, height + 2)
        local_states(e, [xp[:, r], xp[:, r + 1]], jnp.where(e == 0, 0, 2), True)

    def near_halo(i, _):
        e = edge(i)

        @pl.when(jnp.where(i == 0, jnp.logical_not(cross), has_outer))
        def _():
            s = jnp.where(e == 0, 0, 1)
            remote(
                xp.at[:, pl.ds(2, 2)], xp.at[:, pl.ds(0, 2)], row_s.at[0], row_r.at[s], (g, h, k)
            ).wait_recv()
            add_halo(e)

        return 0

    def near_halos():
        lax.fori_loop(0, 2, near_halo, 0)

    late = both(k >= q, jnp.logical_or(m != half - 2, k >= q + 2))
    pl.when(late)(near_halos)

    def relay():
        pl.semaphore_wait(far_sem, 1)
        piece(0).wait_recv()
        forward.start()

    pl.when(both(jnp.logical_not(cross), jnp.logical_not(early)))(relay)

    def pass_on(e):
        chain_copy(e).wait_recv()
        carried = cin[e].astype(F32)

        @pl.when(nx)
        def _():
            send_row(e, prod[steps - 1 : steps, :] * carried + last[e])

        return carried

    def link_edge(i, _):
        e = edge(i)
        for o in range(2):
            pass_on(e + o)

            @pl.when(both(nx, jnp.logical_not(held_back(i))))
            def _():
                send_edge(e, o)

        return 0

    def link(e, _):
        finish(e, pass_on(e))
        return 0

    @pl.when(pv)
    def _():
        lax.fori_loop(0, 2, link_edge, 0)
        lax.fori_loop(2, height, link, 0)

    @pl.when(head)
    def _():
        def plain(e, _):
            for t in range(steps):
                st[e, t] = u[e, t].astype(BF16)
            return 0

        lax.fori_loop(2, height, plain, 0)

    @pl.when(both(cross, early))
    def _():
        pl.semaphore_wait(far_ok, 1)
        direct.start()
        tell_relays()

        @pl.when(nx)
        def _():
            for o in range(2):
                send_edge(edge(0), o)

    pl.when(both(jnp.logical_not(cross), early))(relay)

    def trim(first, rows):
        @pl.when(jnp.logical_not(lf))
        def _():
            st[pl.ds(first, rows), :, 0:PAD] = jnp.zeros((rows, steps, PAD, chans), BF16)

        @pl.when(jnp.logical_not(rt))
        def _():
            st[pl.ds(first, rows), :, cols - PAD : cols] = jnp.zeros((rows, steps, PAD, chans), BF16)

    def mix(r):
        y = conv_pair([st[r + j] for j in range(4)], wo, 0)
        for o in range(2):
            mixed = y[:, PAD : PAD + width, o * chans : (o + 1) * chans]
            held = xp[:, r + o + 2].astype(F32)[:, PAD : PAD + width]
            out[:, r + o] = (held + jax.nn.gelu(mixed)).astype(BF16)

    trim(2, height - 2)

    def inner_out(i, _):
        mix(2 * i)
        return 0

    lax.fori_loop(1, height // 2 - 1, inner_out, 0)
    pl.when(jnp.logical_not(late))(near_halos)

    def edge_out(i, _):
        e = edge(1 - i)
        top = e == 0

        @pl.when(both(cross, i == 1))
        def _():
            for j in range(half):
                landing(j, rb, pc_s.at[0]).wait_recv()
            add_halo(e)

        s = jnp.where(top, 0, 2)
        for o in range(2):
            pl.when(both(pv, jnp.where(top, up, dn)))(
                remote(cout.at[0], cx.at[0], bd_s.at[0], bd_r.at[s + o], (g, h, k)).wait_recv
            )
            finish(e + o, cin[e + o].astype(F32) + cx[s + o].astype(F32))
        trim(e, 2)

        @pl.when(jnp.logical_not(jnp.where(top, up, dn)))
        def _():
            st[jnp.where(top, 0, ext - 1)] = jnp.zeros((steps, cols, chans), BF16)

        mix(jnp.where(top, 0, height - 2))
        return 0

    lax.fori_loop(0, 2, edge_out, 0)

    pl.when(lf)(to_lf.wait_send)
    pl.when(rt)(to_rt.wait_send)
    pl.when(up_near)(to_up.wait_send)
    pl.when(dn_near)(to_dn.wait_send)

    @pl.when(cross)
    def _():
        for i in range(half - 1):
            piece(i).wait_send()
        direct.wait_send()

    @pl.when(jnp.logical_not(cross))
    def _():
        forward.wait_send()

    for o in range(2):
        pl.when(both(nx, dn))(down_copy(o).wait_send)
        pl.when(both(nx, up))(up_copy(o).wait_send)

    @pl.when(nx)
    def _():
        def sent(e, _):
            chain_copy(e).wait_send()
            return 0

        lax.fori_loop(0, ext, sent, 0)


def on_device(frames, in_weight, out_weight, decays):
    steps, height, width, chans = frames.shape
    cols, ext = width + 2 * PAD, height + 2
    half = lax.axis_size("gx") // 2
    dma = pltpu.SemaphoreType.DMA
    flag = pltpu.SemaphoreType.REGULAR
    hbm = pl.BlockSpec(memory_space=pltpu.HBM)
    return pl.pallas_call(
        kernel,
        out_shape=jax.ShapeDtypeStruct(frames.shape, BF16),
        in_specs=[hbm, hbm, hbm, hbm],
        out_specs=pl.BlockSpec(memory_space=pltpu.VMEM),
        scratch_shapes=[
            pltpu.VMEM((steps, height + 4, cols, chans), BF16),
            pltpu.VMEM(in_weight.shape, BF16),
            pltpu.VMEM(out_weight.shape, BF16),
            pltpu.VMEM(decays.shape, F32),
            pltpu.VMEM((4 * chans, 6 * chans), BF16),
            pltpu.VMEM((4 * chans, 6 * chans), BF16),
            pltpu.VMEM((ext, steps, cols, chans), F32),
            pltpu.VMEM((ext, steps, cols, chans), BF16),
            pltpu.VMEM((steps, chans), F32),
            pltpu.VMEM((ext, cols, chans), BF16),
            pltpu.VMEM((ext, cols, chans), BF16),
            pltpu.VMEM((4, cols, chans), BF16),
            pltpu.VMEM((steps // half, 2, cols, chans), BF16),
            pltpu.VMEM((ext, cols, chans), F32),
            flag, flag, dma((4,)), dma((2,)), dma((2,)), dma((2,)), dma((2,)),
            dma((ext,)), dma((ext,)), dma((4,)), dma((4,)), dma((half,)), dma((half,)), dma((1,)), dma((1,)),
        ],
        compiler_params=pltpu.CompilerParams(
            collective_id=0, has_side_effects=True, vmem_limit_bytes=28 << 20
        ),
        name="layer",
    )(frames, in_weight, out_weight, decays)


def solution(mesh):
    placed = (P("ta", "gx", "gy", None), P(), P(), P("ta", None))
    return jax.shard_map(
        on_device, mesh=mesh, in_specs=placed, out_specs=P("ta", "gx", "gy", None), check_vma=False
    )
```

time: 60.4 us -> 48.8 us (0.81)
  the two profiles are of different devices: /device:TPU:55 before, /device:TPU:502 now
where the time goes in v2:
time: 48.8 us; the launch traced here: 48.6 us
  Pallas kernels  43.8 us (90%)
  local copies, waits for them, and re-layouts  4.81 us (10%)
    pallas_call x1, Pallas kernels, on_device(): pl.pallas_call(kernel, out_shape=jax.ShapeDtypeStruct(frames.shape, BF16)...  43.8 us
    unnamed x9, local copies, waits for them, and re-layouts  4.81 us

profile of v2, /device:TPU:502, one launch (start us, length us, event | category | flops | bytes accessed | tf_op | source)
XLA Modules:
  0.0 48.6 jit_solution(3792175264022864357)
XLA Ops:
  0.0 0.0 copy-start
  0.0 1.2 %copy-done = bf16[8,8,64,128]{3,2,1,0:T(8,128)(2,1)S(1)} copy-done((bf16[8,8,64,128]{3,2,1,0:T(8,128)(2,1)S(1)}, bf16[8,8,64,128]{3,2,1,0:T(8,128)(2,1)}, u32[]{:S(2)}) %copy-start) | copy-done | bytes 1048600
  1.2 0.0 copy-start.1
  1.2 1.0 %copy-done.1 = bf16[3,3,128,128]{3,2,1,0:T(8,128)(2,1)S(1)} copy-done((bf16[3,3,128,128]{3,2,1,0:T(8,128)(2,1)S(1)}, bf16[3,3,128,128]{3,2,1,0:T(8,128)(2,1)}, u32[]{:S(2)}) %copy-start.1) | copy-done | bytes 294936
  2.2 0.0 copy-start.2
  2.2 1.0 %copy-done.2 = bf16[3,3,128,128]{3,2,1,0:T(8,128)(2,1)S(1)} copy-done((bf16[3,3,128,128]{3,2,1,0:T(8,128)(2,1)S(1)}, bf16[3,3,128,128]{3,2,1,0:T(8,128)(2,1)}, u32[]{:S(2)}) %copy-start.2) | copy-done | bytes 294936
  3.1 0.0 copy-start.3
  3.2 0.7 %copy-done.3 = f32[8,128]{1,0:T(8,128)S(1)} copy-done((f32[8,128]{1,0:T(8,128)S(1)}, f32[8,128]{1,0:T(8,128)}, u32[]{:S(2)}) %copy-start.3) | copy-done | bytes 4120
  3.8 43.8 %layer.1 = bf16[8,8,64,128]{3,2,1,0:T(8,128)(2,1)S(1)} custom-call(bf16[8,8,64,128]{3,2,1,0:T(8,128)(2,1)S(1)} %copy-done, bf16[3,3,128,128]{3,2,1,0:T(8,128)(2,1)S(1)} %copy-done.1, bf16[3,3,128,128]{3,2,1,0:T(8,128)(2,1)S(1)} %copy-done.2, f32[8,128]{1,0:T(8,128)S(1)} %copy-done.3), custom_call_target="tpu_custom_call" | custom-call | tf_op jit(solution)/shard_map/layer/pallas_call | solution.py:447
  47.6 1.0 %copy.6 = bf16[8,8,64,128]{3,2,1,0:T(8,128)(2,1)} copy(bf16[8,8,64,128]{3,2,1,0:T(8,128)(2,1)S(1)} %layer.1) | data formatting | bytes 2097152
Async XLA Ops:
  0.0 1.2 %copy-start = (bf16[8,8,64,128]{3,2,1,0:T(8,128)(2,1)S(1)}, bf16[8,8,64,128]{3,2,1,0:T(8,128)(2,1)}, u32[]{:S(2)}) copy-start(bf16[8,8,64,128]{3,2,1,0:T(8,128)(2,1)} %x_hbm.1) | copy-start | bytes 3145732
  1.2 1.0 %copy-start.1 = (bf16[3,3,128,128]{3,2,1,0:T(8,128)(2,1)S(1)}, bf16[3,3,128,128]{3,2,1,0:T(8,128)(2,1)}, u32[]{:S(2)}) copy-start(bf16[3,3,128,128]{3,2,1,0:T(8,128)(2,1)} %wi_hbm.1) | copy-start | bytes 884740
  2.2 1.0 %copy-start.2 = (bf16[3,3,128,128]{3,2,1,0:T(8,128)(2,1)S(1)}, bf16[3,3,128,128]{3,2,1,0:T(8,128)(2,1)}, u32[]{:S(2)}) copy-start(bf16[3,3,128,128]{3,2,1,0:T(8,128)(2,1)} %wo_hbm.1) | copy-start | bytes 884740
  3.1 0.7 %copy-start.3 = (f32[8,128]{1,0:T(8,128)S(1)}, f32[8,128]{1,0:T(8,128)}, u32[]{:S(2)}) copy-start(f32[8,128]{1,0:T(8,128)} %dec_hbm.1) | copy-start | bytes 12292

commit v3 on v2

--- a/solution.py
+++ b/solution.py
@@ -8,7 +8,7 @@
 from jax.sharding import PartitionSpec as P
 
 MESH = pl.DeviceIdType.MESH
-PAD = 8
+PAD = 4
 F32 = jnp.float32
 BF16 = jnp.bfloat16
 
@@ -44,8 +44,9 @@
 
 
 def kernel(
-    x_hbm, wi_hbm, wo_hbm, dec_hbm, out, xp, wi_ref, wo_ref, dec, wi, wo, u, st, prod, cin, cout, cx, rb, last,
+    x_hbm, wi_hbm, wo_hbm, dec_hbm, out, xp, wi_ref, wo_ref, dec, wi, wo, u, st, prod, cin, cout, cx, rb, last, cin2, cx2, before,
     far_ok, far_sem, loc, col_s, col_r, row_s, row_r, ch_s, ch_r, bd_s, bd_r, pc_s, pc_r, rl_s, rl_r,
+    c2_s, c2_r, b2_s, b2_r, pr_s, pr_r,
 ):
     steps, height, width, chans = x_hbm.shape
     cols = width + 2 * PAD
@@ -56,6 +57,9 @@
     up, dn = g > 0, g < 2 * half - 1
     lf, rt = h > 0, h < lax.axis_size("gy") - 1
     pv, nx = k > 0, k < lax.axis_size("ta") - 1
+    odd = lax.rem(k, 2) == 1
+    even = jnp.logical_not(odd)
+    pv2, nx2 = both(odd, k > 2), both(odd, k < lax.axis_size("ta") - 2)
     low = g < half
     m = jnp.where(low, g, 2 * half - 1 - g)
     cross = m == half - 1
@@ -78,6 +82,8 @@
         (has_outer, (outer, h, k)), (jnp.logical_not(cross), (inner, h, k)),
         (both(has_outer, pv), (outer, h, k - 1)), (both(pv, jnp.logical_not(cross)), (inner, h, k - 1)),
         (m < half - 2, (jnp.where(low, half - 1, half), h, k)),
+        (both(cross, pv2), (far, h, collector(k - 2))), (pv2, (g, h, k - 2)),
+        (both(has_outer, pv2), (outer, h, k - 2)), (both(pv2, jnp.logical_not(cross)), (inner, h, k - 2)),
     ]
     for there, device in signals:
 
@@ -116,6 +122,19 @@
     def _():
         cin[...] = jnp.zeros(cin.shape, BF16)
 
+    @pl.when(jnp.logical_not(pv2))
+    def _():
+        cin2[...] = jnp.zeros(cin2.shape, BF16)
+        before[...] = jnp.zeros(before.shape, F32)
+
+    @pl.when(jnp.logical_not(both(pv2, up)))
+    def _():
+        cx2[0:2] = jnp.zeros((2, cols, chans), BF16)
+
+    @pl.when(jnp.logical_not(both(pv2, dn)))
+    def _():
+        cx2[2:4] = jnp.zeros((2, cols, chans), BF16)
+
     @pl.when(jnp.logical_not(both(pv, up)))
     def _():
         cx[0:2] = jnp.zeros((2, cols, chans), BF16)
@@ -127,8 +146,10 @@
     def num(flag):
         return flag.astype(jnp.int32)
 
-    count = num(lf) + num(rt) + (1 + num(nx)) * (num(has_outer) + num(jnp.logical_not(cross))) + num(nx)
-    count = count + num(cross) * (half - 2) + num(both(cross, jnp.logical_not(early))) * (4 + num(nx))
+    beside = num(has_outer) + num(jnp.logical_not(cross))
+    count = num(lf) + num(rt) + beside + (num(nx) + num(nx2)) * (1 + beside) + num(cross) * (half - 2)
+    second = num(nx2) + num(both(lax.rem(k + q, 2) == 1, k - q + 2 < 2 * q))
+    count = count + num(both(cross, jnp.logical_not(early))) * (4 + num(nx) + second)
     pl.semaphore_wait(bar, count)
 
     def tell_relays():
@@ -227,13 +248,33 @@
     def up_copy(o):
         return remote(cout.at[o], cx.at[2 + o], bd_s.at[2 + o], bd_r.at[2 + o], (g - 1, h, k + 1))
 
+    def chain_copy2(e):
+        return remote(cout.at[e], cin2.at[e], c2_s.at[e], c2_r.at[e], (g, h, k + 2))
+
+    def down_copy2(o):
+        return remote(cout.at[height + o], cx2.at[o], b2_s.at[o], b2_r.at[o], (g + 1, h, k + 2))
+
+    def up_copy2(o):
+        return remote(cout.at[o], cx2.at[2 + o], b2_s.at[2 + o], b2_r.at[2 + o], (g - 1, h, k + 2))
+
+    product = remote(prod, before, pr_s.at[0], pr_r.at[0], (g, h, k + 1))
+    pl.when(both(even, both(pv, nx)))(product.start)
+
     def send_row(e, value):
         cout[e] = value.astype(BF16)
+        pl.when(nx2)(chain_copy2(e).start)
         chain_copy(e).start()
 
     def send_edge(e, o):
-        pl.when(both(e == 0, up))(up_copy(o).start)
-        pl.when(both(e > 0, dn))(down_copy(o).start)
+        for there, first, second in ((both(e == 0, up), up_copy, up_copy2), (both(e > 0, dn), down_copy, down_copy2)):
+
+            @pl.when(there)
+            def _(first=first, second=second):
+                pl.when(nx2)(second(o).start)
+                first(o).start()
+
+    def carry(e):
+        return cin[e].astype(F32) + before[steps - 1 : steps, :] * cin2[e].astype(F32)
 
     def finish(e, carried):
         for t in range(steps):
@@ -243,16 +284,15 @@
         return jnp.where((i == 0) == low, height, 0)
 
     def held_back(i):
-        return both(both(cross, early), i == 0)
-
-    head = jnp.logical_not(pv)
+        return both(both(cross, both(early, k <= 2)), i == 0)
+
 
     def own_edge(i, _):
         e = edge(i)
         r = jnp.where(e == 0, 2, height)
         local_states(e, [xp[:, r], xp[:, r + 1]], jnp.where(e == 0, 2, 0), False)
 
-        @pl.when(both(head, nx))
+        @pl.when(both(even, nx))
         def _():
             for o in range(2):
                 send_row(e + o, last[e + o])
@@ -266,7 +306,7 @@
         e = 2 * i
         local_states(e, [xp[:, e + j] for j in range(4)], 0, False)
 
-        @pl.when(both(head, nx))
+        @pl.when(both(even, nx))
         def _():
             for o in range(2):
                 send_row(e + o, last[e + o])
@@ -295,67 +335,49 @@
     def near_halos():
         lax.fori_loop(0, 2, near_halo, 0)
 
-    late = both(k >= q, jnp.logical_or(m != half - 2, k >= q + 2))
-    pl.when(late)(near_halos)
+    def far_ready():
+        pl.semaphore_wait(far_ok, 1)
+        direct.start()
+        tell_relays()
+
+        @pl.when(both(nx, k <= 2))
+        def _():
+            for o in range(2):
+                send_edge(edge(0), o)
 
     def relay():
         pl.semaphore_wait(far_sem, 1)
         piece(0).wait_recv()
         forward.start()
 
-    pl.when(both(jnp.logical_not(cross), jnp.logical_not(early)))(relay)
+    late = both(k >= q, jnp.logical_or(m != half - 2, k >= q + 2))
+    pl.when(both(both(cross, early), k != 1))(far_ready)
+    pl.when(late)(near_halos)
+    pl.when(both(jnp.logical_not(cross), k != 1))(relay)
+    pl.when(pv2)(product.wait_recv)
 
     def pass_on(e):
         chain_copy(e).wait_recv()
-        carried = cin[e].astype(F32)
-
-        @pl.when(nx)
-        def _():
-            send_row(e, prod[steps - 1 : steps, :] * carried + last[e])
-
-        return carried
+        pl.when(pv2)(chain_copy2(e).wait_recv)
+
+        @pl.when(both(odd, nx))
+        def _():
+            send_row(e, prod[steps - 1 : steps, :] * carry(e) + last[e])
 
     def link_edge(i, _):
         e = edge(i)
         for o in range(2):
             pass_on(e + o)
 
-            @pl.when(both(nx, jnp.logical_not(held_back(i))))
+            @pl.when(both(both(odd, nx), jnp.logical_not(held_back(i))))
             def _():
                 send_edge(e, o)
 
         return 0
 
-    def link(e, _):
-        finish(e, pass_on(e))
-        return 0
-
     @pl.when(pv)
     def _():
         lax.fori_loop(0, 2, link_edge, 0)
-        lax.fori_loop(2, height, link, 0)
-
-    @pl.when(head)
-    def _():
-        def plain(e, _):
-            for t in range(steps):
-                st[e, t] = u[e, t].astype(BF16)
-            return 0
-
-        lax.fori_loop(2, height, plain, 0)
-
-    @pl.when(both(cross, early))
-    def _():
-        pl.semaphore_wait(far_ok, 1)
-        direct.start()
-        tell_relays()
-
-        @pl.when(nx)
-        def _():
-            for o in range(2):
-                send_edge(edge(0), o)
-
-    pl.when(both(jnp.logical_not(cross), early))(relay)
 
     def trim(first, rows):
         @pl.when(jnp.logical_not(lf))
@@ -373,20 +395,21 @@
             held = xp[:, r + o + 2].astype(F32)[:, PAD : PAD + width]
             out[:, r + o] = (held + jax.nn.gelu(mixed)).astype(BF16)
 
-    trim(2, height - 2)
-
-    def inner_out(i, _):
-        mix(2 * i)
-        return 0
-
-    lax.fori_loop(1, height // 2 - 1, inner_out, 0)
-    pl.when(jnp.logical_not(late))(near_halos)
-
-    def edge_out(i, _):
-        e = edge(1 - i)
+    def first_row(j):
+        return jnp.where(low, 2 * j, height - 2 - 2 * j)
+
+    def inner_pair(j):
+        e = first_row(j) + jnp.where(low, 2, 0)
+        for o in range(2):
+            pl.when(pv)(lambda o=o: pass_on(e + o))
+            finish(e + o, carry(e + o))
+        trim(e, 2)
+
+    def edge_pair(i):
+        e = edge(i)
         top = e == 0
 
-        @pl.when(both(cross, i == 1))
+        @pl.when(both(cross, i == 0))
         def _():
             for j in range(half):
                 landing(j, rb, pc_s.at[0]).wait_recv()
@@ -397,17 +420,38 @@
             pl.when(both(pv, jnp.where(top, up, dn)))(
                 remote(cout.at[0], cx.at[0], bd_s.at[0], bd_r.at[s + o], (g, h, k)).wait_recv
             )
-            finish(e + o, cin[e + o].astype(F32) + cx[s + o].astype(F32))
+            pl.when(both(pv2, jnp.where(top, up, dn)))(
+                remote(cout.at[0], cx2.at[0], b2_s.at[0], b2_r.at[s + o], (g, h, k)).wait_recv
+            )
+            beyond = cx[s + o].astype(F32) + before[steps - 1 : steps, :] * cx2[s + o].astype(F32)
+            finish(e + o, carry(e + o) + beyond)
         trim(e, 2)
 
         @pl.when(jnp.logical_not(jnp.where(top, up, dn)))
         def _():
             st[jnp.where(top, 0, ext - 1)] = jnp.zeros((steps, cols, chans), BF16)
 
-        mix(jnp.where(top, 0, height - 2))
+    pairs = height // 2
+
+    @pl.when(jnp.logical_not(late))
+    def _():
+        def one(j, _):
+            inner_pair(j)
+            return 0
+
+        lax.fori_loop(0, pairs - 1, one, 0)
+
+    pl.when(both(cross, k == 1))(far_ready)
+    pl.when(both(jnp.logical_not(cross), k == 1))(relay)
+    pl.when(jnp.logical_not(late))(near_halos)
+
+    def row_pair(j, _):
+        pl.when(both(late, j < pairs - 1))(lambda: inner_pair(j))
+        pl.when(jnp.logical_or(j == 0, j == pairs - 1))(lambda: edge_pair(jnp.where(j == 0, 1, 0)))
+        mix(first_row(j))
         return 0
 
-    lax.fori_loop(0, 2, edge_out, 0)
+    lax.fori_loop(0, pairs, row_pair, 0)
 
     pl.when(lf)(to_lf.wait_send)
     pl.when(rt)(to_rt.wait_send)
@@ -427,11 +471,15 @@
     for o in range(2):
         pl.when(both(nx, dn))(down_copy(o).wait_send)
         pl.when(both(nx, up))(up_copy(o).wait_send)
+        pl.when(both(nx2, dn))(down_copy2(o).wait_send)
+        pl.when(both(nx2, up))(up_copy2(o).wait_send)
+    pl.when(both(even, both(pv, nx)))(product.wait_send)
 
     @pl.when(nx)
     def _():
         def sent(e, _):
             chain_copy(e).wait_send()
+            pl.when(nx2)(chain_copy2(e).wait_send)
             return 0
 
         lax.fori_loop(0, ext, sent, 0)
@@ -444,6 +492,10 @@
     dma = pltpu.SemaphoreType.DMA
     flag = pltpu.SemaphoreType.REGULAR
     hbm = pl.BlockSpec(memory_space=pltpu.HBM)
+    args = [
+        pltpu.with_memory_space_constraint(arg, pltpu.HBM)
+        for arg in (frames, in_weight, out_weight, decays)
+    ]
     return pl.pallas_call(
         kernel,
         out_shape=jax.ShapeDtypeStruct(frames.shape, BF16),
@@ -464,14 +516,18 @@
             pltpu.VMEM((4, cols, chans), BF16),
             pltpu.VMEM((steps // half, 2, cols, chans), BF16),
             pltpu.VMEM((ext, cols, chans), F32),
+            pltpu.VMEM((ext, cols, chans), BF16),
+            pltpu.VMEM((4, cols, chans), BF16),
+            pltpu.VMEM((steps, chans), F32),
             flag, flag, dma((4,)), dma((2,)), dma((2,)), dma((2,)), dma((2,)),
             dma((ext,)), dma((ext,)), dma((4,)), dma((4,)), dma((half,)), dma((half,)), dma((1,)), dma((1,)),
+            dma((ext,)), dma((ext,)), dma((4,)), dma((4,)), dma((1,)), dma((1,)),
         ],
         compiler_params=pltpu.CompilerParams(
             collective_id=0, has_side_effects=True, vmem_limit_bytes=28 << 20
         ),
         name="layer",
-    )(frames, in_weight, out_weight, decays)
+    )(*args)
 
 
 def solution(mesh):

time: 48.8 us -> 40.7 us (0.83)
  the two profiles are of different devices: /device:TPU:502 before, /device:TPU:141 now
where the time goes in v3:
time: 40.7 us; the launch traced here: 40.5 us
  Pallas kernels  39.5 us (97%)
  local copies, waits for them, and re-layouts  0.97 us (2%)
    pallas_call x1, Pallas kernels, on_device(): pl.pallas_call(kernel, out_shape=jax.ShapeDtypeStruct(frames.shape, BF16)...  39.5 us
    unnamed x1, local copies, waits for them, and re-layouts  0.97 us

profile of v3, /device:TPU:141, one launch (start us, length us, event | category | flops | bytes accessed | tf_op | source)
XLA Modules:
  0.0 40.5 jit_solution(8100142594268521682)
XLA Ops:
  0.0 39.5 %layer.1 = bf16[8,8,64,128]{3,2,1,0:T(8,128)(2,1)S(1)} custom-call(bf16[8,8,64,128]{3,2,1,0:T(8,128)(2,1)} %x_hbm.1, bf16[3,3,128,128]{3,2,1,0:T(8,128)(2,1)} %wi_hbm.1, bf16[3,3,128,128]{3,2,1,0:T(8,128)(2,1)} %wo_hbm.1, f32[8,128]{1,0:T(8,128)} %dec_hbm.1), custom_call_target="tpu_custom_call" | custom-call | tf_op jit(solution)/shard_map/layer/pallas_call | solution.py:499
  39.5 1.0 %copy.6 = bf16[8,8,64,128]{3,2,1,0:T(8,128)(2,1)} copy(bf16[8,8,64,128]{3,2,1,0:T(8,128)(2,1)S(1)} %layer.1) | data formatting | bytes 2097152

commit v4 on v3

--- a/solution.py
+++ b/solution.py
@@ -44,9 +44,9 @@
 
 
 def kernel(
-    x_hbm, wi_hbm, wo_hbm, dec_hbm, out, xp, wi_ref, wo_ref, dec, wi, wo, u, st, prod, cin, cout, cx, rb, last, cin2, cx2, before,
+    x_hbm, wi_hbm, wo_hbm, dec_hbm, out, xp, wi_ref, wo_ref, dec, wi, wo, u, st, prod, cin, cout, cx, rb, last, cin2, cx2, before, cc,
     far_ok, far_sem, loc, col_s, col_r, row_s, row_r, ch_s, ch_r, bd_s, bd_r, pc_s, pc_r, rl_s, rl_r,
-    c2_s, c2_r, b2_s, b2_r, pr_s, pr_r,
+    c2_s, c2_r, b2_s, b2_r, pr_s, pr_r, nb_s,
 ):
     steps, height, width, chans = x_hbm.shape
     cols = width + 2 * PAD
@@ -66,10 +66,13 @@
     inner, outer = jnp.where(low, g + 1, g - 1), jnp.where(low, g - 1, g + 1)
     has_outer = m > 0
     far = 2 * half - 1 - g
+    mine = jnp.where(low, half - 1, half)
     up_near, dn_near = both(up, g != half), both(dn, g != half - 1)
 
     q = lax.axis_size("ta") // 2
     early = k < q
+    shifted = both(low, both(pv, early))
+    here = jnp.logical_not(shifted)
 
     def collector(at):
         return jnp.where(at < q, at + q, at)
@@ -80,10 +83,8 @@
         (both(cross, early), (g, h, k + q)),
         (lf, (g, h - 1, k)), (rt, (g, h + 1, k)), (pv, (g, h, k - 1)),
         (has_outer, (outer, h, k)), (jnp.logical_not(cross), (inner, h, k)),
-        (both(has_outer, pv), (outer, h, k - 1)), (both(pv, jnp.logical_not(cross)), (inner, h, k - 1)),
-        (m < half - 2, (jnp.where(low, half - 1, half), h, k)),
+        (both(m < half - 2, here), (mine, h, k)), (both(both(low, k < q - 1), jnp.logical_not(cross)), (mine, h, k + 1)),
         (both(cross, pv2), (far, h, collector(k - 2))), (pv2, (g, h, k - 2)),
-        (both(has_outer, pv2), (outer, h, k - 2)), (both(pv2, jnp.logical_not(cross)), (inner, h, k - 2)),
     ]
     for there, device in signals:
 
@@ -127,13 +128,13 @@
         cin2[...] = jnp.zeros(cin2.shape, BF16)
         before[...] = jnp.zeros(before.shape, F32)
 
-    @pl.when(jnp.logical_not(both(pv2, up)))
-    def _():
-        cx2[0:2] = jnp.zeros((2, cols, chans), BF16)
-
-    @pl.when(jnp.logical_not(both(pv2, dn)))
-    def _():
-        cx2[2:4] = jnp.zeros((2, cols, chans), BF16)
+    @pl.when(jnp.logical_not(both(pv2, cross)))
+    def _():
+        cx2[...] = jnp.zeros(cx2.shape, BF16)
+
+    @pl.when(both(pv2, cross))
+    def _():
+        cx2[pl.ds(jnp.where(low, 0, 2), 2)] = jnp.zeros((2, cols, chans), BF16)
 
     @pl.when(jnp.logical_not(both(pv, up)))
     def _():
@@ -147,15 +148,17 @@
         return flag.astype(jnp.int32)
 
     beside = num(has_outer) + num(jnp.logical_not(cross))
-    count = num(lf) + num(rt) + beside + (num(nx) + num(nx2)) * (1 + beside) + num(cross) * (half - 2)
+    count = num(lf) + num(rt) + beside + num(nx) + num(nx2) + num(cross) * (half - 2 + num(shifted))
     second = num(nx2) + num(both(lax.rem(k + q, 2) == 1, k - q + 2 < 2 * q))
     count = count + num(both(cross, jnp.logical_not(early))) * (4 + num(nx) + second)
     pl.semaphore_wait(bar, count)
 
+    slot, back = jnp.where(shifted, 0, 1), jnp.where(shifted, k - 1, k)
+
     def tell_relays():
         for i in range(half - 1):
             pl.semaphore_signal(
-                far_sem, inc=1, device_id=(jnp.where(low, i, 2 * half - 1 - i), h, k), device_id_type=MESH
+                far_sem.at[slot], inc=1, device_id=(jnp.where(low, i, 2 * half - 1 - i), h, back), device_id_type=MESH
             )
 
     @pl.when(both(cross, jnp.logical_not(early)))
@@ -187,18 +190,21 @@
 
     def piece(i):
         return remote(
-            xp.at[pl.ds(span * i, span), pl.ds(leave, 2)], rb, pc_s.at[i], rl_r.at[0],
-            (jnp.where(low, i, 2 * half - 1 - i), h, k),
+            xp.at[pl.ds(span * i, span), pl.ds(leave, 2)], rb.at[slot], pc_s.at[i], rl_r.at[slot],
+            (jnp.where(low, i, 2 * half - 1 - i), h, back),
         )
 
-    def landing(i, src, ss):
+    def landing(i, src, ss, at):
         return remote(
             src, xp.at[pl.ds(span * i, span), pl.ds(land, 2)], ss, pc_r.at[i],
-            (jnp.where(low, half, half - 1), h, k),
+            (jnp.where(low, half, half - 1), h, at),
         )
 
-    direct = landing(half - 1, xp.at[pl.ds(span * (half - 1), span), pl.ds(leave, 2)], pc_s.at[half - 1])
-    forward = landing(m, rb, rl_s.at[0])
+    direct = landing(half - 1, xp.at[pl.ds(span * (half - 1), span), pl.ds(leave, 2)], pc_s.at[half - 1], k)
+
+    def forward(i):
+        return landing(m, rb.at[i], rl_s.at[i], k + 1 - i)
+
 
     pl.when(lf)(to_lf.start)
     pl.when(rt)(to_rt.start)
@@ -242,20 +248,34 @@
     def chain_copy(e):
         return remote(cout.at[e], cin.at[e], ch_s.at[e], ch_r.at[e], (g, h, k + 1))
 
-    def down_copy(o):
-        return remote(cout.at[height + o], cx.at[o], bd_s.at[o], bd_r.at[o], (g + 1, h, k + 1))
-
-    def up_copy(o):
-        return remote(cout.at[o], cx.at[2 + o], bd_s.at[2 + o], bd_r.at[2 + o], (g - 1, h, k + 1))
-
     def chain_copy2(e):
         return remote(cout.at[e], cin2.at[e], c2_s.at[e], c2_r.at[e], (g, h, k + 2))
 
-    def down_copy2(o):
-        return remote(cout.at[height + o], cx2.at[o], b2_s.at[o], b2_r.at[o], (g + 1, h, k + 2))
-
-    def up_copy2(o):
-        return remote(cout.at[o], cx2.at[2 + o], b2_s.at[2 + o], b2_r.at[2 + o], (g - 1, h, k + 2))
+    def edge(i):
+        return jnp.where((i == 0) == low, height, 0)
+
+    theirs = jnp.where(low, 0, 2)
+
+    def far_copy(o):
+        return remote(
+            cout.at[edge(0) + o], cx.at[theirs + o], bd_s.at[o], bd_r.at[theirs + o], (far, h, k + 1)
+        )
+
+    def far_copy2(o):
+        return remote(
+            cout.at[edge(0) + o], cx2.at[theirs + o], b2_s.at[o], b2_r.at[theirs + o], (far, h, k + 2)
+        )
+
+    def near_copy(i, o):
+        top = edge(i) == 0
+        there = jnp.where(top, 2, 0) + o
+        return remote(
+            cc.at[2 * i + o], cx.at[there], nb_s.at[2 * i + o], bd_r.at[there],
+            (jnp.where(top, g - 1, g + 1), h, k),
+        )
+
+    def beside_at(i):
+        return both(pv, jnp.where(i == 0, jnp.logical_not(cross), has_outer))
 
     product = remote(prod, before, pr_s.at[0], pr_r.at[0], (g, h, k + 1))
     pl.when(both(even, both(pv, nx)))(product.start)
@@ -265,13 +285,9 @@
         pl.when(nx2)(chain_copy2(e).start)
         chain_copy(e).start()
 
-    def send_edge(e, o):
-        for there, first, second in ((both(e == 0, up), up_copy, up_copy2), (both(e > 0, dn), down_copy, down_copy2)):
-
-            @pl.when(there)
-            def _(first=first, second=second):
-                pl.when(nx2)(second(o).start)
-                first(o).start()
+    def send_far(o):
+        pl.when(nx2)(far_copy2(o).start)
+        far_copy(o).start()
 
     def carry(e):
         return cin[e].astype(F32) + before[steps - 1 : steps, :] * cin2[e].astype(F32)
@@ -280,11 +296,9 @@
         for t in range(steps):
             st[e, t] = (u[e, t] + prod[t : t + 1, :] * carried).astype(BF16)
 
-    def edge(i):
-        return jnp.where((i == 0) == low, height, 0)
-
-    def held_back(i):
-        return both(both(cross, both(early, k <= 2)), i == 0)
+    def far_now(i):
+        waits = jnp.logical_or(both(early, both(even, k <= 2)), both(low, k == 1))
+        return both(both(cross, jnp.logical_not(waits)), i == 0)
 
 
     def own_edge(i, _):
@@ -296,7 +310,7 @@
         def _():
             for o in range(2):
                 send_row(e + o, last[e + o])
-                pl.when(jnp.logical_not(held_back(i)))(lambda o=o: send_edge(e, o))
+                pl.when(far_now(i))(lambda o=o: send_far(o))
 
         return 0
 
@@ -340,20 +354,27 @@
         direct.start()
         tell_relays()
 
-        @pl.when(both(nx, k <= 2))
+        @pl.when(both(nx, jnp.logical_or(both(even, k <= 2), wait_far)))
         def _():
             for o in range(2):
-                send_edge(edge(0), o)
-
-    def relay():
-        pl.semaphore_wait(far_sem, 1)
-        piece(0).wait_recv()
-        forward.start()
+                send_far(o)
+
+    def relay(i):
+        pl.semaphore_wait(far_sem.at[i], 1)
+        remote(
+            xp.at[pl.ds(0, span), pl.ds(0, 2)], rb.at[i], pc_s.at[0], rl_r.at[i], (g, h, k)
+        ).wait_recv()
+        forward(i).start()
 
     late = both(k >= q, jnp.logical_or(m != half - 2, k >= q + 2))
-    pl.when(both(both(cross, early), k != 1))(far_ready)
+    wait_far = both(k == 1, low)
+    pl.when(both(both(cross, early), jnp.logical_not(wait_far)))(far_ready)
     pl.when(late)(near_halos)
-    pl.when(both(jnp.logical_not(cross), k != 1))(relay)
+    straight = jnp.logical_not(cross)
+    pl.when(both(straight, both(here, k != 1)))(lambda: relay(1))
+    serve = both(straight, both(low, k < q - 1))
+    after = odd
+    pl.when(both(serve, jnp.logical_not(after)))(lambda: relay(0))
     pl.when(pv2)(product.wait_recv)
 
     def pass_on(e):
@@ -369,15 +390,20 @@
         for o in range(2):
             pass_on(e + o)
 
-            @pl.when(both(both(odd, nx), jnp.logical_not(held_back(i))))
+            pl.when(both(both(odd, nx), far_now(i)))(lambda o=o: send_far(o))
+
+            @pl.when(beside_at(i))
             def _():
-                send_edge(e, o)
+                cc[2 * i + o] = carry(e + o).astype(BF16)
+                near_copy(i, o).start()
 
         return 0
 
     @pl.when(pv)
     def _():
         lax.fori_loop(0, 2, link_edge, 0)
+
+    pl.when(both(straight, both(here, k == 1)))(lambda: relay(1))
 
     def trim(first, rows):
         @pl.when(jnp.logical_not(lf))
@@ -412,7 +438,7 @@
         @pl.when(both(cross, i == 0))
         def _():
             for j in range(half):
-                landing(j, rb, pc_s.at[0]).wait_recv()
+                landing(j, rb.at[0], pc_s.at[0], k).wait_recv()
             add_halo(e)
 
         s = jnp.where(top, 0, 2)
@@ -420,7 +446,7 @@
             pl.when(both(pv, jnp.where(top, up, dn)))(
                 remote(cout.at[0], cx.at[0], bd_s.at[0], bd_r.at[s + o], (g, h, k)).wait_recv
             )
-            pl.when(both(pv2, jnp.where(top, up, dn)))(
+            pl.when(both(pv2, both(cross, i == 0)))(
                 remote(cout.at[0], cx2.at[0], b2_s.at[0], b2_r.at[s + o], (g, h, k)).wait_recv
             )
             beyond = cx[s + o].astype(F32) + before[steps - 1 : steps, :] * cx2[s + o].astype(F32)
@@ -441,8 +467,8 @@
 
         lax.fori_loop(0, pairs - 1, one, 0)
 
-    pl.when(both(cross, k == 1))(far_ready)
-    pl.when(both(jnp.logical_not(cross), k == 1))(relay)
+    pl.when(both(cross, wait_far))(far_ready)
+    pl.when(both(serve, after))(lambda: relay(0))
     pl.when(jnp.logical_not(late))(near_halos)
 
     def row_pair(j, _):
@@ -464,15 +490,14 @@
             piece(i).wait_send()
         direct.wait_send()
 
-    @pl.when(jnp.logical_not(cross))
-    def _():
-        forward.wait_send()
+    pl.when(serve)(lambda: forward(0).wait_send())
+    pl.when(both(straight, here))(lambda: forward(1).wait_send())
 
     for o in range(2):
-        pl.when(both(nx, dn))(down_copy(o).wait_send)
-        pl.when(both(nx, up))(up_copy(o).wait_send)
-        pl.when(both(nx2, dn))(down_copy2(o).wait_send)
-        pl.when(both(nx2, up))(up_copy2(o).wait_send)
+        pl.when(both(cross, nx))(far_copy(o).wait_send)
+        pl.when(both(cross, nx2))(far_copy2(o).wait_send)
+        for i in range(2):
+            pl.when(beside_at(i))(near_copy(i, o).wait_send)
     pl.when(both(even, both(pv, nx)))(product.wait_send)
 
     @pl.when(nx)
@@ -514,14 +539,15 @@
             pltpu.VMEM((ext, cols, chans), BF16),
             pltpu.VMEM((ext, cols, chans), BF16),
             pltpu.VMEM((4, cols, chans), BF16),
-            pltpu.VMEM((steps // half, 2, cols, chans), BF16),
+            pltpu.VMEM((2, steps // half, 2, cols, chans), BF16),
             pltpu.VMEM((ext, cols, chans), F32),
             pltpu.VMEM((ext, cols, chans), BF16),
             pltpu.VMEM((4, cols, chans), BF16),
             pltpu.VMEM((steps, chans), F32),
-            flag, flag, dma((4,)), dma((2,)), dma((2,)), dma((2,)), dma((2,)),
-            dma((ext,)), dma((ext,)), dma((4,)), dma((4,)), dma((half,)), dma((half,)), dma((1,)), dma((1,)),
-            dma((ext,)), dma((ext,)), dma((4,)), dma((4,)), dma((1,)), dma((1,)),
+            pltpu.VMEM((4, cols, chans), BF16),
+            flag, pltpu.SemaphoreType.REGULAR((2,)), dma((4,)), dma((2,)), dma((2,)), dma((2,)), dma((2,)),
+            dma((ext,)), dma((ext,)), dma((4,)), dma((4,)), dma((half,)), dma((half,)), dma((2,)), dma((2,)),
+            dma((ext,)), dma((ext,)), dma((2,)), dma((4,)), dma((1,)), dma((1,)), dma((4,)),
         ],
         compiler_params=pltpu.CompilerParams(
             collective_id=0, has_side_effects=True, vmem_limit_bytes=28 << 20

time: 40.7 us -> 39.7 us (0.975)
  the two profiles are of different devices: /device:TPU:141 before, /device:TPU:39 now
where the time goes in v4:
time: 39.7 us; the launch traced here: 39.5 us
  Pallas kernels  38.5 us (97%)
  local copies, waits for them, and re-layouts  0.97 us (2%)
    pallas_call x1, Pallas kernels, on_device(): pl.pallas_call(kernel, out_shape=jax.ShapeDtypeStruct(frames.shape, BF16)...  38.5 us
    unnamed x1, local copies, waits for them, and re-layouts  0.97 us

profile of v4, /device:TPU:39, one launch (start us, length us, event | category | flops | bytes accessed | tf_op | source)
XLA Modules:
  0.0 39.5 jit_solution(11616880408994178268)
XLA Ops:
  0.0 38.5 %layer.1 = bf16[8,8,64,128]{3,2,1,0:T(8,128)(2,1)S(1)} custom-call(bf16[8,8,64,128]{3,2,1,0:T(8,128)(2,1)} %x_hbm.1, bf16[3,3,128,128]{3,2,1,0:T(8,128)(2,1)} %wi_hbm.1, bf16[3,3,128,128]{3,2,1,0:T(8,128)(2,1)} %wo_hbm.1, f32[8,128]{1,0:T(8,128)} %dec_hbm.1), custom_call_target="tpu_custom_call" | custom-call | tf_op jit(solution)/shard_map/layer/pallas_call | solution.py:524
  38.6 1.0 %copy.6 = bf16[8,8,64,128]{3,2,1,0:T(8,128)(2,1)} copy(bf16[8,8,64,128]{3,2,1,0:T(8,128)(2,1)S(1)} %layer.1) | data formatting | bytes 2097152

commit v5 on v4

--- a/solution.py
+++ b/solution.py
@@ -186,21 +186,22 @@
     to_dn = remote(
         xp.at[:, pl.ds(height, 2)], xp.at[:, pl.ds(0, 2)], row_s.at[1], row_r.at[0], (g + 1, h, k)
     )
+    used = pl.ds(PAD - 2, width + 4)
     leave, land = jnp.where(low, height, 2), jnp.where(low, 0, height + 2)
 
     def piece(i):
         return remote(
-            xp.at[pl.ds(span * i, span), pl.ds(leave, 2)], rb.at[slot], pc_s.at[i], rl_r.at[slot],
+            xp.at[pl.ds(span * i, span), pl.ds(leave, 2), used], rb.at[slot], pc_s.at[i], rl_r.at[slot],
             (jnp.where(low, i, 2 * half - 1 - i), h, back),
         )
 
     def landing(i, src, ss, at):
         return remote(
-            src, xp.at[pl.ds(span * i, span), pl.ds(land, 2)], ss, pc_r.at[i],
+            src, xp.at[pl.ds(span * i, span), pl.ds(land, 2), used], ss, pc_r.at[i],
             (jnp.where(low, half, half - 1), h, at),
         )
 
-    direct = landing(half - 1, xp.at[pl.ds(span * (half - 1), span), pl.ds(leave, 2)], pc_s.at[half - 1], k)
+    direct = landing(half - 1, xp.at[pl.ds(span * (half - 1), span), pl.ds(leave, 2), used], pc_s.at[half - 1], k)
 
     def forward(i):
         return landing(m, rb.at[i], rl_s.at[i], k + 1 - i)
@@ -246,10 +247,10 @@
                 last[e + o] = state
 
     def chain_copy(e):
-        return remote(cout.at[e], cin.at[e], ch_s.at[e], ch_r.at[e], (g, h, k + 1))
+        return remote(cout.at[e, used], cin.at[e, used], ch_s.at[e], ch_r.at[e], (g, h, k + 1))
 
     def chain_copy2(e):
-        return remote(cout.at[e], cin2.at[e], c2_s.at[e], c2_r.at[e], (g, h, k + 2))
+        return remote(cout.at[e, used], cin2.at[e, used], c2_s.at[e], c2_r.at[e], (g, h, k + 2))
 
     def edge(i):
         return jnp.where((i == 0) == low, height, 0)
@@ -362,7 +363,7 @@
     def relay(i):
         pl.semaphore_wait(far_sem.at[i], 1)
         remote(
-            xp.at[pl.ds(0, span), pl.ds(0, 2)], rb.at[i], pc_s.at[0], rl_r.at[i], (g, h, k)
+            xp.at[pl.ds(0, span), pl.ds(0, 2), used], rb.at[i], pc_s.at[0], rl_r.at[i], (g, h, k)
         ).wait_recv()
         forward(i).start()
 
@@ -539,7 +540,7 @@
             pltpu.VMEM((ext, cols, chans), BF16),
             pltpu.VMEM((ext, cols, chans), BF16),
             pltpu.VMEM((4, cols, chans), BF16),
-            pltpu.VMEM((2, steps // half, 2, cols, chans), BF16),
+            pltpu.VMEM((2, steps // half, 2, width + 4, chans), BF16),
             pltpu.VMEM((ext, cols, chans), F32),
             pltpu.VMEM((ext, cols, chans), BF16),
             pltpu.VMEM((4, cols, chans), BF16),

time: 39.7 us -> 39.6 us (level)
  the two profiles are of different devices: /device:TPU:39 before, /device:TPU:55 now
where the time goes in v5:
time: 39.6 us; the launch traced here: 39.4 us
  Pallas kernels  38.4 us (97%)
  local copies, waits for them, and re-layouts  0.97 us (2%)
    pallas_call x1, Pallas kernels, on_device(): pl.pallas_call(kernel, out_shape=jax.ShapeDtypeStruct(frames.shape, BF16)...  38.4 us
    unnamed x1, local copies, waits for them, and re-layouts  0.97 us

profile of v5, /device:TPU:55, one launch (start us, length us, event | category | flops | bytes accessed | tf_op | source)
XLA Modules:
  0.0 39.4 jit_solution(4022681645691131122)
XLA Ops:
  0.0 38.4 %layer.1 = bf16[8,8,64,128]{3,2,1,0:T(8,128)(2,1)S(1)} custom-call(bf16[8,8,64,128]{3,2,1,0:T(8,128)(2,1)} %x_hbm.1, bf16[3,3,128,128]{3,2,1,0:T(8,128)(2,1)} %wi_hbm.1, bf16[3,3,128,128]{3,2,1,0:T(8,128)(2,1)} %wo_hbm.1, f32[8,128]{1,0:T(8,128)} %dec_hbm.1), custom_call_target="tpu_custom_call" | custom-call | tf_op jit(solution)/shard_map/layer/pallas_call | solution.py:525
  38.5 1.0 %copy.6 = bf16[8,8,64,128]{3,2,1,0:T(8,128)(2,1)} copy(bf16[8,8,64,128]{3,2,1,0:T(8,128)(2,1)S(1)} %layer.1) | data formatting | bytes 2097152

commit v6 on v5

--- a/solution.py
+++ b/solution.py
@@ -259,19 +259,19 @@
 
     def far_copy(o):
         return remote(
-            cout.at[edge(0) + o], cx.at[theirs + o], bd_s.at[o], bd_r.at[theirs + o], (far, h, k + 1)
+            cout.at[edge(0) + o, used], cx.at[theirs + o, used], bd_s.at[o], bd_r.at[theirs + o], (far, h, k + 1)
         )
 
     def far_copy2(o):
         return remote(
-            cout.at[edge(0) + o], cx2.at[theirs + o], b2_s.at[o], b2_r.at[theirs + o], (far, h, k + 2)
+            cout.at[edge(0) + o, used], cx2.at[theirs + o, used], b2_s.at[o], b2_r.at[theirs + o], (far, h, k + 2)
         )
 
     def near_copy(i, o):
         top = edge(i) == 0
         there = jnp.where(top, 2, 0) + o
         return remote(
-            cc.at[2 * i + o], cx.at[there], nb_s.at[2 * i + o], bd_r.at[there],
+            cc.at[2 * i + o, used], cx.at[there, used], nb_s.at[2 * i + o], bd_r.at[there],
             (jnp.where(top, g - 1, g + 1), h, k),
         )
 
@@ -316,6 +316,20 @@
         return 0
 
     lax.fori_loop(0, 2, own_edge, 0)
+    wait_far = both(k == 1, low)
+    ahead = both(jnp.logical_not(low), both(early, pv))
+
+    def far_ready():
+        pl.semaphore_wait(far_ok, 1)
+        direct.start()
+        tell_relays()
+
+        @pl.when(both(nx, jnp.logical_or(both(even, k <= 2), wait_far)))
+        def _():
+            for o in range(2):
+                send_far(o)
+
+    pl.when(both(cross, ahead))(far_ready)
 
     def own_inner(i, _):
         e = 2 * i
@@ -349,16 +363,6 @@
 
     def near_halos():
         lax.fori_loop(0, 2, near_halo, 0)
-
-    def far_ready():
-        pl.semaphore_wait(far_ok, 1)
-        direct.start()
-        tell_relays()
-
-        @pl.when(both(nx, jnp.logical_or(both(even, k <= 2), wait_far)))
-        def _():
-            for o in range(2):
-                send_far(o)
 
     def relay(i):
         pl.semaphore_wait(far_sem.at[i], 1)
@@ -368,8 +372,7 @@
         forward(i).start()
 
     late = both(k >= q, jnp.logical_or(m != half - 2, k >= q + 2))
-    wait_far = both(k == 1, low)
-    pl.when(both(both(cross, early), jnp.logical_not(wait_far)))(far_ready)
+    pl.when(both(both(cross, early), jnp.logical_not(jnp.logical_or(wait_far, ahead))))(far_ready)
     pl.when(late)(near_halos)
     straight = jnp.logical_not(cross)
     pl.when(both(straight, both(here, k != 1)))(lambda: relay(1))
@@ -445,10 +448,10 @@
         s = jnp.where(top, 0, 2)
         for o in range(2):
             pl.when(both(pv, jnp.where(top, up, dn)))(
-                remote(cout.at[0], cx.at[0], bd_s.at[0], bd_r.at[s + o], (g, h, k)).wait_recv
+                remote(cout.at[0, used], cx.at[0, used], bd_s.at[0], bd_r.at[s + o], (g, h, k)).wait_recv
             )
             pl.when(both(pv2, both(cross, i == 0)))(
-                remote(cout.at[0], cx2.at[0], b2_s.at[0], b2_r.at[s + o], (g, h, k)).wait_recv
+                remote(cout.at[0, used], cx2.at[0, used], b2_s.at[0], b2_r.at[s + o], (g, h, k)).wait_recv
             )
             beyond = cx[s + o].astype(F32) + before[steps - 1 : steps, :] * cx2[s + o].astype(F32)
             finish(e + o, carry(e + o) + beyond)

time: 39.6 us -> 38 us (0.960)
  the two profiles are of different devices: /device:TPU:55 before, /device:TPU:47 now
where the time goes in v6:
time: 38 us; the launch traced here: 37.9 us
  Pallas kernels  36.9 us (97%)
  local copies, waits for them, and re-layouts  0.97 us (3%)
    pallas_call x1, Pallas kernels, on_device(): pl.pallas_call(kernel, out_shape=jax.ShapeDtypeStruct(frames.shape, BF16)...  36.9 us
    unnamed x1, local copies, waits for them, and re-layouts  0.97 us

profile of v6, /device:TPU:47, one launch (start us, length us, event | category | flops | bytes accessed | tf_op | source)
XLA Modules:
  0.0 37.9 jit_solution(6136501977645829640)
XLA Ops:
  0.0 36.9 %layer.1 = bf16[8,8,64,128]{3,2,1,0:T(8,128)(2,1)S(1)} custom-call(bf16[8,8,64,128]{3,2,1,0:T(8,128)(2,1)} %x_hbm.1, bf16[3,3,128,128]{3,2,1,0:T(8,128)(2,1)} %wi_hbm.1, bf16[3,3,128,128]{3,2,1,0:T(8,128)(2,1)} %wo_hbm.1, f32[8,128]{1,0:T(8,128)} %dec_hbm.1), custom_call_target="tpu_custom_call" | custom-call | tf_op jit(solution)/shard_map/layer/pallas_call | solution.py:528
  36.9 1.0 %copy.6 = bf16[8,8,64,128]{3,2,1,0:T(8,128)(2,1)} copy(bf16[8,8,64,128]{3,2,1,0:T(8,128)(2,1)S(1)} %layer.1) | data formatting | bytes 2097152
